TPU v7x, 768 devices: a whole 4x8x12 slice. The times are simulated.
768 devices in a mesh: section: 8 (over y_lo, core), dp: 96 (over y_hi, x, z).
Axes of the slice: x: 4, y: 8 (y_hi: 2, y_lo: 4; y = y_hi * 4 + y_lo), z: 12, core: 2. Of those that a mesh axis runs over, the one named last changes fastest.
Arguments:
- queries: bfloat16 [8, 12288, 8192], P('section', 'dp'), may hold values from -48 to 48
- image_kv: bfloat16 [8, 2, 768, 1024], P(None, None, ('section', 'dp')), may hold values from -4 to 4
- visible: int32 [12288], P('dp'), may hold values from 0 to 768, as said below
- gate: float32 [8], P('section'), may hold values from 0.3 to 2
Outputs:
- cross_out: bfloat16 [8, 12288, 8192], P('section', 'dp')
Inputs may be any that keep to these rules, and one draw needn't show every extreme that they name: `visible`: every value is a multiple of 192; the last token of each aligned block of 128 text tokens sees all 768 image tokens.
All inputs are finite; a program needn't handle non-finite values.
Results may differ from a plain program's by a relative error of at most 0.0065.
Values may be sent and summed in bfloat16 or wider, within the bound.
No kernel may reach another device: no remote copies, remote signals or barrier semaphores. Data moves between devices by JAX's collectives and lax.ppermute only.
A program may use at most 64 MiB of HBM per device.

v0:
```python
import math

import jax
import jax.numpy as jnp
from jax import lax
from jax.sharding import PartitionSpec as P

H = 64
KVH = 8
HD = 128


block_rows = 128


def global_position(position, dp_count, section_count, img_dev):
    per_dp = section_count * img_dev
    source_section = position % per_dp // img_dev
    source_dp = position // per_dp
    return source_section * (dp_count * img_dev) + source_dp * img_dev + position % img_dev


def attend(stats, keys_flat, vals_flat, glob, query, seen):
    top, denom, acc = stats
    count = keys_flat.shape[0]
    kv_heads = query.shape[1]
    head_size = query.shape[3]
    keys = keys_flat.reshape(count, kv_heads, head_size)
    vals = vals_flat.reshape(count, kv_heads, head_size)
    live = glob[None, :] < seen[:, None]
    scores = jnp.einsum("tkgd,nkd->kgtn", query, keys, preferred_element_type=jnp.float32)
    scores = scores / jnp.sqrt(jnp.float32(head_size))
    capped = jnp.where(live, scores, -1e30)
    top_new = jnp.maximum(top, jnp.max(capped, axis=-1))
    expo = jnp.where(live, jnp.exp(capped - top_new[..., None]), 0.0)
    factor = jnp.exp(top - top_new)
    denom = denom * factor + jnp.sum(expo, axis=-1)
    acc = acc * factor[..., None] + jnp.einsum(
        "kgtn,nkd->kgtd", expo.astype(jnp.bfloat16), vals, preferred_element_type=jnp.float32
    )
    return (top_new, denom, acc)


def body(queries, image_kv, visible, gate):
    section_count = lax.axis_size("section")
    dp_count = lax.axis_size("dp")
    img_dev = image_kv.shape[2]
    rows = queries.shape[1]
    kv_heads = KVH
    groups = H // KVH
    width = image_kv.shape[3]
    query = queries[0].reshape(rows, kv_heads, groups, HD)
    mine = lax.all_to_all(image_kv, "section", split_axis=0, concat_axis=2, tiled=True)
    start_top = jnp.full((kv_heads, groups, rows), -1e30, jnp.float32)
    start_denom = jnp.zeros((kv_heads, groups, rows), jnp.float32)
    start_acc = jnp.zeros((kv_heads, groups, rows, HD), jnp.float32)
    stats = (start_top, start_denom, start_acc)
    whole = lax.all_gather(mine, "dp", axis=2, tiled=True)
    total = whole.shape[2]
    block = math.gcd(total, block_rows)
    count = total // block
    blocked = jnp.moveaxis(whole.reshape(2, count, block, width), 1, 0)

    def scan_step(carry, pair):
        glob = global_position(
            pair[1] + jnp.arange(block, dtype=jnp.int32), dp_count, section_count, img_dev
        )
        return (attend(carry, pair[0][0], pair[0][1], glob, query, visible), None)

    starts = jnp.arange(count, dtype=jnp.int32) * block
    final, unused = lax.scan(scan_step, stats, (blocked, starts))
    top, denom, acc = final
    result = acc / jnp.where(denom > 0, denom, 1.0)[..., None]
    result = jnp.transpose(result, (2, 0, 1, 3)).reshape(rows, H * HD)
    result = jnp.where((visible > 0)[:, None], result, 0.0) * jnp.tanh(gate[0])
    return result.astype(jnp.bfloat16)[None]


def solution(mesh):
    in_specs = (
        P("section", "dp", None),
        P(None, None, ("section", "dp"), None),
        P("dp"),
        P("section"),
    )
    out_specs = P("section", "dp", None)
    return jax.shard_map(body, mesh=mesh, in_specs=in_specs, out_specs=out_specs, check_vma=False)
```

profile of v0, /device:TPU:4, one launch (start us, length us, event | category | flops | bytes accessed | tf_op | source)
XLA Modules:
  0.0 328.9 jit_solution(3213440120957396417)
XLA Ops:
  6.5 10.6 %all_to_all.18 = bf16[8,2,1,1024]{3,1,2,0:T(2,128)(2,1)S(1)} all-to-all(bf16[8,2,1,1024]{3,1,2,0:T(2,128)(2,1)} %param.7), channel_id=1, replica_groups=mesh['section'=8,'dp'=96] {'section'}, dimensions={0} | all-to-all | bytes 65536 | tf_op jit(solution)/shard_map/all_to_all | solution.py:53
  17.2 0.6 copy.34
  17.8 4.1 %copy.19 = bf16[1,128,8192]{1,2,0:T(8,128)(2,1)} copy(bf16[1,128,8192]{2,1,0:T(8,128)(2,1)} %param.6) | data formatting | bytes 4194304 | tf_op args[0]
  21.9 3.0 copy.21
  25.7 192.3 %all-gather.3.cloned.1.call-done = bf16[1,2,768,1,1024]{4,2,1,3,0:T(8,128)(2,1)} async-done(((bf16[1,2,8,1,1024]{4,2,1,3,0:T(8,128)(2,1)}), bf16[1,2,768,1,1024]{4,2,1,3,0:T(8,128)(2,1)}) %all-gather.3.cloned.1.call-update) | async-done | bytes 3145744 | tf_op jit(solution)/shard_map/all_gather | solution.py:58
  218.0 87.9 %while.18 = (s32[]{:T(128)}, f32[8,8,128]{2,1,0:T(8,128)S(1)}, f32[8,8,128]{2,1,0:T(8,128)S(1)}, f32[8,8,128,128]{3,2,1,0:T(8,128)}, s32[6]{0:T(128)S(1)}, /*ind...) while((s32[]{:T(128)}, f32[8,8,128]{2,1,0:T(8,128)S(1)}, ...), condition=%wide.region_3.4_spmd.clone, body=%wide.region_0.3_spmd.clone.sunk | while | flops 553708288 | bytes 26281628 | solution.py:71
  218.0 0.6 dynamic_slice.19
  218.5 0.6 fusion.32
  219.1 0.1 broadcast_compare_fusion.3
  219.2 1.1 constant_dynamic-slice_fusion.3
  220.3 0.2 copy.37
  220.5 2.8 fusion.33
  223.3 3.3 %fusion.34 = f32[8,8,128]{2,1,0:T(8,128)S(1)} fusion(f32[8,128,128,8]{2,1,3,0:T(8,128)} %get-tuple-element.271, f32[8,8,128]{2,1,0:T(8,128)S(1)} %select_maximum_fusion.2, pred[128,128]{0,1:T(8,128)(4,1)S(1)} %broadcast_compare_fusion.3), kind=kLoop, calls=%fused_computation.6.clone.1 | loop fusion | flops 5234688 | bytes 4276224 | tf_op jit(solution)/shard_map/while/body/eval_jaxpr/reduce_sum | solution.py:37
  226.6 0.2 copy.38
  226.8 5.2 %fusion.36 = f32[8,8,128,128]{3,2,1,0:T(8,128)} fusion(f32[8,8,128,128]{3,2,1,0:T(8,128)} %get-tuple-element.289, bf16[128,8,128,1]{0,2,3,1:T(8,128)(2,1)S(1)} %bitcast.57, f32[8,128,128,8]{2,1,3,0:T(8,128)} %get-tuple-element.271, f32[8,8,128]{2,1,0:T(8,128)S(1)} %get-tuple-element.274, f32[8,8,128]{2,1,0:T(8,128)S(1)} %select_maximum_fusion.2, ...), kind=kOutput, calls=%fused_computation.2.clone.1 | convolution fusion | flops 276824064 | bytes 12926977 | tf_op jit(solution)/shard_map/while/body/eval_jaxpr/kgtn,nkd->kgtd/dot_general | solution.py:38
  232.0 0.6 dynamic_slice.19
  232.6 0.6 fusion.32
  233.2 0.1 broadcast_compare_fusion.3
  233.3 1.1 constant_dynamic-slice_fusion.3
  234.3 0.2 copy.37
  234.5 2.8 fusion.33
  237.3 3.3 %fusion.34 = f32[8,8,128]{2,1,0:T(8,128)S(1)} fusion(f32[8,128,128,8]{2,1,3,0:T(8,128)} %get-tuple-element.271, f32[8,8,128]{2,1,0:T(8,128)S(1)} %select_maximum_fusion.2, pred[128,128]{0,1:T(8,128)(4,1)S(1)} %broadcast_compare_fusion.3), kind=kLoop, calls=%fused_computation.6.clone.1 | loop fusion | flops 5234688 | bytes 4276224 | tf_op jit(solution)/shard_map/while/body/eval_jaxpr/reduce_sum | solution.py:37
  240.7 0.2 copy.38
  240.8 5.9 %fusion.36 = f32[8,8,128,128]{3,2,1,0:T(8,128)} fusion(f32[8,8,128,128]{3,2,1,0:T(8,128)} %get-tuple-element.289, bf16[128,8,128,1]{0,2,3,1:T(8,128)(2,1)S(1)} %bitcast.57, f32[8,128,128,8]{2,1,3,0:T(8,128)} %get-tuple-element.271, f32[8,8,128]{2,1,0:T(8,128)S(1)} %get-tuple-element.274, f32[8,8,128]{2,1,0:T(8,128)S(1)} %select_maximum_fusion.2, ...), kind=kOutput, calls=%fused_computation.2.clone.1 | convolution fusion | flops 276824064 | bytes 12926977 | tf_op jit(solution)/shard_map/while/body/eval_jaxpr/kgtn,nkd->kgtd/dot_general | solution.py:38
  246.8 0.6 dynamic_slice.19
  247.4 0.6 fusion.32
  248.0 0.1 broadcast_compare_fusion.3
  248.0 1.1 constant_dynamic-slice_fusion.3
  249.1 0.2 copy.37
  249.3 2.8 fusion.33
  252.1 3.3 %fusion.34 = f32[8,8,128]{2,1,0:T(8,128)S(1)} fusion(f32[8,128,128,8]{2,1,3,0:T(8,128)} %get-tuple-element.271, f32[8,8,128]{2,1,0:T(8,128)S(1)} %select_maximum_fusion.2, pred[128,128]{0,1:T(8,128)(4,1)S(1)} %broadcast_compare_fusion.3), kind=kLoop, calls=%fused_computation.6.clone.1 | loop fusion | flops 5234688 | bytes 4276224 | tf_op jit(solution)/shard_map/while/body/eval_jaxpr/reduce_sum | solution.py:37
  255.4 0.2 copy.38
  255.6 5.9 %fusion.36 = f32[8,8,128,128]{3,2,1,0:T(8,128)} fusion(f32[8,8,128,128]{3,2,1,0:T(8,128)} %get-tuple-element.289, bf16[128,8,128,1]{0,2,3,1:T(8,128)(2,1)S(1)} %bitcast.57, f32[8,128,128,8]{2,1,3,0:T(8,128)} %get-tuple-element.271, f32[8,8,128]{2,1,0:T(8,128)S(1)} %get-tuple-element.274, f32[8,8,128]{2,1,0:T(8,128)S(1)} %select_maximum_fusion.2, ...), kind=kOutput, calls=%fused_computation.2.clone.1 | convolution fusion | flops 276824064 | bytes 12926977 | tf_op jit(solution)/shard_map/while/body/eval_jaxpr/kgtn,nkd->kgtd/dot_general | solution.py:38
  261.6 0.6 dynamic_slice.19
  262.1 0.6 fusion.32
  262.7 0.1 broadcast_compare_fusion.3
  262.8 1.1 constant_dynamic-slice_fusion.3
  263.9 0.2 copy.37
  264.1 2.8 fusion.33
  266.9 3.3 %fusion.34 = f32[8,8,128]{2,1,0:T(8,128)S(1)} fusion(f32[8,128,128,8]{2,1,3,0:T(8,128)} %get-tuple-element.271, f32[8,8,128]{2,1,0:T(8,128)S(1)} %select_maximum_fusion.2, pred[128,128]{0,1:T(8,128)(4,1)S(1)} %broadcast_compare_fusion.3), kind=kLoop, calls=%fused_computation.6.clone.1 | loop fusion | flops 5234688 | bytes 4276224 | tf_op jit(solution)/shard_map/while/body/eval_jaxpr/reduce_sum | solution.py:37
  270.2 0.2 copy.38
  270.4 5.9 %fusion.36 = f32[8,8,128,128]{3,2,1,0:T(8,128)} fusion(f32[8,8,128,128]{3,2,1,0:T(8,128)} %get-tuple-element.289, bf16[128,8,128,1]{0,2,3,1:T(8,128)(2,1)S(1)} %bitcast.57, f32[8,128,128,8]{2,1,3,0:T(8,128)} %get-tuple-element.271, f32[8,8,128]{2,1,0:T(8,128)S(1)} %get-tuple-element.274, f32[8,8,128]{2,1,0:T(8,128)S(1)} %select_maximum_fusion.2, ...), kind=kOutput, calls=%fused_computation.2.clone.1 | convolution fusion | flops 276824064 | bytes 12926977 | tf_op jit(solution)/shard_map/while/body/eval_jaxpr/kgtn,nkd->kgtd/dot_general | solution.py:38
  276.3 0.6 dynamic_slice.19
  276.9 0.6 fusion.32
  277.5 0.1 broadcast_compare_fusion.3
  277.6 1.1 constant_dynamic-slice_fusion.3
  278.7 0.2 copy.37
  278.8 2.8 fusion.33
  281.7 3.3 %fusion.34 = f32[8,8,128]{2,1,0:T(8,128)S(1)} fusion(f32[8,128,128,8]{2,1,3,0:T(8,128)} %get-tuple-element.271, f32[8,8,128]{2,1,0:T(8,128)S(1)} %select_maximum_fusion.2, pred[128,128]{0,1:T(8,128)(4,1)S(1)} %broadcast_compare_fusion.3), kind=kLoop, calls=%fused_computation.6.clone.1 | loop fusion | flops 5234688 | bytes 4276224 | tf_op jit(solution)/shard_map/while/body/eval_jaxpr/reduce_sum | solution.py:37
  285.0 0.2 copy.38
  285.2 5.9 %fusion.36 = f32[8,8,128,128]{3,2,1,0:T(8,128)} fusion(f32[8,8,128,128]{3,2,1,0:T(8,128)} %get-tuple-element.289, bf16[128,8,128,1]{0,2,3,1:T(8,128)(2,1)S(1)} %bitcast.57, f32[8,128,128,8]{2,1,3,0:T(8,128)} %get-tuple-element.271, f32[8,8,128]{2,1,0:T(8,128)S(1)} %get-tuple-element.274, f32[8,8,128]{2,1,0:T(8,128)S(1)} %select_maximum_fusion.2, ...), kind=kOutput, calls=%fused_computation.2.clone.1 | convolution fusion | flops 276824064 | bytes 12926977 | tf_op jit(solution)/shard_map/while/body/eval_jaxpr/kgtn,nkd->kgtd/dot_general | solution.py:38
  291.1 0.6 dynamic_slice.19
  291.7 0.6 fusion.32
  292.3 0.1 broadcast_compare_fusion.3
  292.4 1.1 constant_dynamic-slice_fusion.3
  293.4 0.2 copy.37
  293.6 2.8 fusion.33
  296.4 3.3 %fusion.34 = f32[8,8,128]{2,1,0:T(8,128)S(1)} fusion(f32[8,128,128,8]{2,1,3,0:T(8,128)} %get-tuple-element.271, f32[8,8,128]{2,1,0:T(8,128)S(1)} %select_maximum_fusion.2, pred[128,128]{0,1:T(8,128)(4,1)S(1)} %broadcast_compare_fusion.3), kind=kLoop, calls=%fused_computation.6.clone.1 | loop fusion | flops 5234688 | bytes 4276224 | tf_op jit(solution)/shard_map/while/body/eval_jaxpr/reduce_sum | solution.py:37
  299.8 0.2 copy.38
  299.9 5.9 %fusion.36 = f32[8,8,128,128]{3,2,1,0:T(8,128)} fusion(f32[8,8,128,128]{3,2,1,0:T(8,128)} %get-tuple-element.289, bf16[128,8,128,1]{0,2,3,1:T(8,128)(2,1)S(1)} %bitcast.57, f32[8,128,128,8]{2,1,3,0:T(8,128)} %get-tuple-element.271, f32[8,8,128]{2,1,0:T(8,128)S(1)} %get-tuple-element.274, f32[8,8,128]{2,1,0:T(8,128)S(1)} %select_maximum_fusion.2, ...), kind=kOutput, calls=%fused_computation.2.clone.1 | convolution fusion | flops 276824064 | bytes 12926977 | tf_op jit(solution)/shard_map/while/body/eval_jaxpr/kgtn,nkd->kgtd/dot_general | solution.py:38
  305.9 2.9 divide_bitcast_fusion
  308.8 4.4 %copy.22 = f32[128,8,8,128]{3,2,1,0:T(8,128)} copy(f32[128,8,8,128]{3,0,2,1:T(8,128)S(1)} %divide_bitcast_fusion) | data formatting | bytes 8388608 | tf_op jit(solution)/shard_map/transpose | solution.py:74
  313.2 4.9 %reshape.92 = f32[1,128,8192]{2,1,0:T(8,128)} reshape(f32[128,8,8,128]{3,2,1,0:T(8,128)} %copy.22) | data formatting | bytes 8388608 | tf_op jit(solution)/shard_map/reshape | solution.py:74
  318.1 4.0 %multiply_convert_fusion = bf16[1,128,8192]{2,1,0:T(8,128)(2,1)} fusion(f32[1,128,8192]{2,1,0:T(8,128)} %reshape.92, f32[]{:T(128)} %bitcast.6, pred[128]{0:T(512)(128)(4,1)S(1)} %broadcast_compare_fusion.1), kind=kLoop, calls=%fused_computation.29 | loop fusion | flops 3145728 | bytes 6291588 | tf_op jit(solution)/shard_map/convert_element_type | solution.py:76
  (28 shorter events, 0.2 us)
Async XLA Ops:
  6.5 211.4 %all-gather.3.cloned.1.call-start = ((), (), s32[]{:S(2)}) async-start(), calls=%async_computation.1 | async-start | bytes 3178496 | tf_op jit(solution)/shard_map/all_gather | solution.py:58
  17.8 7.8 %copy-start = (s32[128]{0:T(128)S(1)}, s32[128]{0:T(128)}, u32[]{:S(2)}) copy-start(s32[128]{0:T(128)} %param.8) | copy-start | bytes 1540
Sparse Core Ops, SparseCore 0:
  17.9 200.0 all-gather.2
where the time goes:
time: 330 us; the launch traced here: 329 us
  waiting for transfers between devices  192 us (58%)
  matrix products  51.9 us (16%)
  other arithmetic  30.8 us (9%)
  local copies, waits for them, and re-layouts  29 us (9%)
  between operations  14.2 us (4%)
  blocking collectives  10.6 us (3%)
    all_gather x1, waiting for transfers between devices, body(): whole = lax.all_gather(mine, 'dp', axis=2, tiled=True)  192 us
    dot_general x6, matrix products, attend(): jnp.einsum('kgtn,nkd->kgtd', expo.astype(jnp.bfloat16), vals, preferred_e...  35 us
    reduce_sum x6, other arithmetic, attend(): denom = denom * factor + jnp.sum(expo, axis=-1)  19.7 us
    dot_general x6, matrix products, attend(): jnp.einsum('tkgd,nkd->kgtn', query, keys, preferred_element_type=jnp.floa...  16.9 us
    all_to_all x1, blocking collectives, body(): lax.all_to_all(image_kv, 'section', split_axis=0, concat_axis=2, tiled=True)  10.6 us
    unnamed x4, local copies, waits for them, and re-layouts  7.11 us
  transfers between devices with their start and end apart: 1, of which 1 were waited for; matrix products, arithmetic and copies ran while one was open for 2% of the time, Pallas kernels for 0%

commit v1 on v0

v1 whole, which is shorter than its diff:
```python
import functools
import math

import jax
import jax.numpy as jnp
from jax import lax
from jax.experimental import pallas as pl
from jax.experimental.pallas import tpu as pltpu
from jax.sharding import Mesh, PartitionSpec as P

H = 64
KVH = 8
HD = 128
G = H // KVH
TILE = 192
NEG = -1e30

FINE = (("ylo", 4), ("core", 2), ("yhi", 2), ("x", 4), ("z", 12))
YRING = ("ylo", "core", "yhi")
LANES = 256
VMEM_BYTES = 16 << 20


def attend_kernel(first, last, gate_ref, q_ref, seen_ref, a_ref, b_ref, *refs):
    refs = list(refs)
    if first:
        old = None
    else:
        old, refs = refs[:3], refs[3:]
    factor = math.log2(math.e) / math.sqrt(HD)
    half = a_ref.shape[0] * a_ref.shape[2]
    count = a_ref.shape[2]
    keys = jnp.concatenate([a_ref[:, 0].reshape(half, HD), b_ref[:, 0].reshape(half, HD)], axis=0)
    vals = jnp.concatenate([a_ref[:, 1].reshape(half, HD), b_ref[:, 1].reshape(half, HD)], axis=0)
    total = 2 * half
    rows = q_ref.shape[1]
    heads = LANES // rows
    tile = lax.broadcasted_iota(jnp.int32, (count, LANES), 0) // (count // 4)
    for c in range(G * rows // LANES):
        lanes = slice(c * LANES, (c + 1) * LANES)
        query = jnp.concatenate(
            [q_ref[0, :, (c * heads + g) * HD : (c * heads + g + 1) * HD] for g in range(heads)], axis=0
        )
        seen = seen_ref[:, lanes]
        score = lax.dot_general(keys, query, (((1,), (1,)), ((), ())), preferred_element_type=jnp.float32)
        live = tile * TILE < seen
        score = jnp.where(live[None], score.reshape(total // count, count, LANES), NEG)
        top = jnp.max(jnp.max(score, axis=0), axis=0, keepdims=True)
        if first:
            new = top
        else:
            new = jnp.maximum(top, old[0][0, :, lanes])
        expo = jnp.exp2((score - new) * factor)
        denom = jnp.sum(jnp.sum(expo, axis=0), axis=0, keepdims=True)
        weights = expo.astype(jnp.bfloat16).reshape(total, LANES)
        acc = lax.dot_general(vals, weights, (((0,), (0,)), ((), ())), preferred_element_type=jnp.float32)
        if not first:
            scale = jnp.exp2((old[0][0, :, lanes] - new) * factor)
            denom = denom + old[1][0, :, lanes] * scale
            acc = acc + old[2][0, :, lanes] * scale
        if last:
            out_ref = refs[0]
            ratio = jnp.where(seen > 0, jnp.tanh(gate_ref[0]) / denom, 0.0)
            result = acc * ratio
            for g in range(heads):
                piece = result[:, g * rows : (g + 1) * rows].T
                out_ref[0, :, (c * heads + g) * HD : (c * heads + g + 1) * HD] = piece.astype(jnp.bfloat16)
        else:
            refs[0][0, :, lanes] = new
            refs[1][0, :, lanes] = denom
            refs[2][0, :, lanes] = acc


def attend(gate, queries, seen, halves, state, last):
    rows = queries.shape[1]
    lanes = G * rows
    steps, _, count, _ = halves[0].shape
    first = state is None
    stat_spec = pl.BlockSpec((1, 1, lanes), lambda k: (k, 0, 0))
    acc_spec = pl.BlockSpec((1, HD, lanes), lambda k: (k, 0, 0))
    state_specs = [stat_spec, stat_spec, acc_spec]
    query_spec = pl.BlockSpec((1, rows, G * HD), lambda k: (0, 0, k))
    half_spec = pl.BlockSpec((steps, 2, count, HD), lambda k: (0, 0, 0, k))
    in_specs = [
        pl.BlockSpec(memory_space=pltpu.SMEM),
        query_spec,
        pl.BlockSpec((1, lanes), lambda k: (0, 0)),
        half_spec,
        half_spec,
    ]
    operands = [gate, queries, seen, *halves]
    aliases = {}
    if not first:
        if not last:
            aliases = {len(operands) + i: i for i in range(3)}
        in_specs += state_specs
        operands += list(state)
    if last:
        out_shape = jax.ShapeDtypeStruct(queries.shape, jnp.bfloat16)
        out_specs = query_spec
    else:
        stat = jax.ShapeDtypeStruct((KVH, 1, lanes), jnp.float32)
        out_shape = [stat, stat, jax.ShapeDtypeStruct((KVH, HD, lanes), jnp.float32)]
        out_specs = state_specs
    total = 2 * steps * count
    return pl.pallas_call(
        functools.partial(attend_kernel, first, last),
        grid=(KVH,),
        in_specs=in_specs,
        out_specs=out_specs,
        out_shape=out_shape,
        input_output_aliases=aliases,
        name="attend",
        compiler_params=pltpu.CompilerParams(vmem_limit_bytes=VMEM_BYTES),
        cost_estimate=pl.CostEstimate(
            flops=4 * H * rows * total * HD,
            bytes_accessed=2 * H * rows * HD + 8 * H * rows * HD,
            transcendentals=H * rows * total,
        ),
    )(*operands)


def body(queries, image_kv, visible, gate):
    layers = image_kv.shape[0]
    ring = lax.axis_size("x")
    seen = jnp.tile(visible, G)[None]
    sent = jnp.repeat(image_kv[:, :, 0], lax.axis_size("yhi"), axis=0)
    mine = lax.all_to_all(sent, YRING, split_axis=0, concat_axis=0, tiled=True)
    mine = jnp.transpose(mine, (1, 0, 2))
    own = lax.all_gather(mine, "z")
    middle = own.shape[0] // 2
    low, high = own[:middle], own[middle:]
    up = [(i, (i + 1) % ring) for i in range(ring)]
    down = [(i, (i - 1) % ring) for i in range(ring)]
    low_left = lax.ppermute(low, "x", up)
    high_right = lax.ppermute(high, "x", down)
    high_left = lax.ppermute(high, "x", up)
    low_right = lax.ppermute(low, "x", down)
    low_far = lax.ppermute(low_left, "x", up)
    high_far = lax.ppermute(high_right, "x", down)
    state = attend(gate, queries, seen, (low, high), None, False)
    state = attend(gate, queries, seen, (low_left, high_right), state, False)
    state = attend(gate, queries, seen, (high_left, low_right), state, False)
    return attend(gate, queries, seen, (low_far, high_far), state, True)


def solution(mesh):
    fine = Mesh(mesh.devices.reshape([n for _, n in FINE]), [a for a, _ in FINE])
    section, dp = ("ylo", "core"), ("yhi", "x", "z")
    in_specs = (
        P(section, dp, None),
        P(None, None, section + dp, None),
        P(dp),
        P(section),
    )
    return jax.shard_map(body, mesh=fine, in_specs=in_specs, out_specs=P(section, dp, None), check_vma=False)
```

time: 330 us -> 113 us (0.34)
  the two profiles are of different devices: /device:TPU:4 before, /device:TPU:8 now
where the time goes in v1:
time: 113 us; the launch traced here: 112 us
  blocking collectives  51.4 us (45%)
  Pallas kernels  35.1 us (31%)
  starting transfers between devices  21.4 us (19%)
  local copies, waits for them, and re-layouts  3.12 us (3%)
    pallas_call x4, Pallas kernels, attend(): pl.pallas_call(functools.partial(attend_kernel, first, last), grid=(KVH,)...  35.1 us
    all_gather x1, blocking collectives, body(): own = lax.all_gather(mine, 'z')  32.5 us
    all_to_all x1, blocking collectives, body(): mine = lax.all_to_all(sent, YRING, split_axis=0, concat_axis=0, tiled=True)  18.9 us
    ppermute x1, starting transfers between devices, body(): low_right = lax.ppermute(low, 'x', down)  4.86 us
    ppermute x1, starting transfers between devices, body(): high_far = lax.ppermute(high_right, 'x', down)  4.73 us
    ppermute x1, starting transfers between devices, body(): high_right = lax.ppermute(high, 'x', down)  3.65 us
    ppermute x1, starting transfers between devices, body(): low_left = lax.ppermute(low, 'x', up)  3.4 us
    ppermute x1, starting transfers between devices, body(): low_far = lax.ppermute(low_left, 'x', up)  2.58 us
  transfers between devices with their start and end apart: 6, of which 1 were waited for; matrix products, arithmetic and copies ran while one was open for 1% of the time, Pallas kernels for 23%

profile of v1, /device:TPU:8, one launch (start us, length us, event | category | flops | bytes accessed | tf_op | source)
XLA Modules:
  0.0 112.4 jit_solution(14039135244357825146)
XLA Ops:
  0.0 0.8 broadcast_in_dim.3
  0.8 18.9 %all_to_all.5 = bf16[16,2,1024]{2,1,0:T(2,128)(2,1)S(1)} all-to-all(bf16[16,2,1024]{2,1,0:T(2,128)(2,1)S(1)} %bitcast.17), channel_id=1, replica_groups=mesh['ylo'=4,'core'=2,'yhi'=2,'x'=4,'z'=12] {'ylo','core','yhi'}, dimensions={0} | all-to-all | bytes 131072 | tf_op jit(solution)/shard_map/all_to_all | solution.py:128
  19.7 32.5 %all-gather = bf16[24,16,1024]{2,1,0:T(8,128)(2,1)S(1)} all-gather(bf16[2,16,1024]{2,1,0:T(8,128)(2,1)S(1)} %copy.12), channel_id=2, replica_groups=mesh['ylo'=4,'core'=2,'yhi'=2,'x'=4,'z'=12] {'z'}, dimensions={0}, use_global_device_ids=true | all-gather | bytes 851968 | tf_op jit(solution)/shard_map/all_gather | solution.py:130
  52.2 0.1 fusion
  52.3 3.4 %collective-permute-start = (bf16[6,2,16,1024]{3,2,1,0:T(8,128)(2,1)S(1)}, bf16[6,2,16,1024]{3,2,1,0:T(8,128)(2,1)S(1)}, u32[]{:S(2)}, u32[]{:S(2)}) collective-permute-start(bf16[6,2,16,1024]{3,2,1,0:T(8,128)(2,1)S(1)} %bitcast.6), channel_id=1, source_target_pairs={{0,12},{12,24},{24,36},{36,0},{1,13},{13,25},{25,37},{37,1},{2,14}... | collective-permute-start | bytes 1179656 | tf_op jit(solution)/shard_map/ppermute | solution.py:135
  55.7 3.7 %collective-permute-start.2 = (bf16[6,2,16,1024]{3,2,1,0:T(8,128)(2,1)S(1)}, bf16[6,2,16,1024]{3,2,1,0:T(8,128)(2,1)S(1)}, u32[]{:S(2)}, u32[]{:S(2)}) collective-permute-start(bf16[6,2,16,1024]{3,2,1,0:T(8,128)(2,1)S(1)} %bitcast.9), channel_id=1, source_target_pairs={{0,36},{12,0},{24,12},{36,24},{1,37},{13,1},{25,13},{37,25},{2,38}... | collective-permute-start | bytes 1179656 | tf_op jit(solution)/shard_map/ppermute | solution.py:136
  59.4 2.2 %collective-permute-start.4 = (bf16[6,2,16,1024]{3,2,1,0:T(8,128)(2,1)S(1)}, bf16[6,2,16,1024]{3,2,1,0:T(8,128)(2,1)S(1)}, u32[]{:S(2)}, u32[]{:S(2)}) collective-permute-start(bf16[6,2,16,1024]{3,2,1,0:T(8,128)(2,1)S(1)} %bitcast.10), channel_id=1, source_target_pairs={{0,12},{12,24},{24,36},{36,0},{1,13},{13,25},{25,37},{37,1},{2,14}... | collective-permute-start | bytes 1179656 | tf_op jit(solution)/shard_map/ppermute | solution.py:137
  61.6 4.9 %collective-permute-start.5 = (bf16[6,2,16,1024]{3,2,1,0:T(8,128)(2,1)S(1)}, bf16[6,2,16,1024]{3,2,1,0:T(8,128)(2,1)S(1)}, u32[]{:S(2)}, u32[]{:S(2)}) collective-permute-start(bf16[6,2,16,1024]{3,2,1,0:T(8,128)(2,1)S(1)} %bitcast.7), channel_id=1, source_target_pairs={{0,36},{12,0},{24,12},{36,24},{1,37},{13,1},{25,13},{37,25},{2,38}... | collective-permute-start | bytes 1179656 | tf_op jit(solution)/shard_map/ppermute | solution.py:138
  66.4 0.6 collective-permute-done.a_ref
  67.0 2.6 %collective-permute-start.1 = (bf16[6,2,16,1024]{3,2,1,0:T(8,128)(2,1)S(1)}, bf16[6,2,16,1024]{3,2,1,0:T(8,128)(2,1)S(1)}, u32[]{:S(2)}, u32[]{:S(2)}) collective-permute-start(bf16[6,2,16,1024]{3,2,1,0:T(8,128)(2,1)S(1)} %collective-permute-done.a_ref), channel_id=1, source_target_pairs={{0,12},{12,24},{24,36},{36,0},{1,13},{13,25},{25,37},{37,1},{2,14}... | collective-permute-start | bytes 1179656 | tf_op jit(solution)/shard_map/ppermute | solution.py:139
  69.6 0.0 collective-permute-done.2.b_ref
  69.6 4.7 %collective-permute-start.3 = (bf16[6,2,16,1024]{3,2,1,0:T(8,128)(2,1)S(1)}, bf16[6,2,16,1024]{3,2,1,0:T(8,128)(2,1)S(1)}, u32[]{:S(2)}, u32[]{:S(2)}) collective-permute-start(bf16[6,2,16,1024]{3,2,1,0:T(8,128)(2,1)S(1)} %collective-permute-done.2.b_ref), channel_id=1, source_target_pairs={{0,36},{12,0},{24,12},{36,24},{1,37},{13,1},{25,13},{37,25},{2,38}... | collective-permute-start | bytes 1179656 | tf_op jit(solution)/shard_map/ppermute | solution.py:140
  75.0 0.7 tile.2
  75.6 0.0 copy-start
  75.6 1.6 %copy-done = bf16[1,128,8192]{2,1,0:T(8,128)(2,1)S(1)} copy-done((bf16[1,128,8192]{2,1,0:T(8,128)(2,1)S(1)}, bf16[1,128,8192]{2,1,0:T(8,128)(2,1)}, u32[]{:S(2)}) %copy-start) | copy-done | bytes 2097176
  77.2 8.3 %attend.4 = (f32[8,1,1024]{2,1,0:T(1,128)S(1)}, f32[8,1,1024]{2,1,0:T(1,128)S(1)}, f32[8,128,1024]{2,1,0:T(8,128)S(1)}) custom-call(f32[1]{0:T(128)S(6)} %copy.19.gate_ref, bf16[1,128,8192]{2,1,0:T(8,128)(2,1)S(1)} %copy-done, s32[1,1024]{1,0:T(1,128)S(1)} %bitcast.12, bf16[6,2,16,1024]{3,2,1,0:T(8,128)(2,1)S(1)} %bitcast.8, ...), custom_call_target="tpu_custom_call" | custom-call | flops 805306368 | bytes 10485760 | tf_op jit(solution)/shard_map/attend/pallas_call | solution.py:106
  85.5 8.5 %attend.5 = (f32[8,1,1024]{2,1,0:T(1,128)S(1)}, f32[8,1,1024]{2,1,0:T(1,128)S(1)}, f32[8,128,1024]{2,1,0:T(8,128)S(1)}) custom-call(f32[1]{0:T(128)S(6)} %copy.19.gate_ref, bf16[1,128,8192]{2,1,0:T(8,128)(2,1)S(1)} %copy-done, s32[1,1024]{1,0:T(1,128)S(1)} %bitcast.13, ...), custom_call_target="tpu_custom_call", output_to_operand_aliasing={{0}: (5, {}), {1}: (6, {}), {2}: (7, {})} | custom-call | flops 805306368 | bytes 10485760 | tf_op jit(solution)/shard_map/attend/pallas_call | solution.py:106
  94.1 0.0 collective-permute-done.4.a_ref
  94.1 0.0 collective-permute-done.5.b_ref
  94.1 8.5 %attend.6 = (f32[8,1,1024]{2,1,0:T(1,128)S(1)}, f32[8,1,1024]{2,1,0:T(1,128)S(1)}, f32[8,128,1024]{2,1,0:T(8,128)S(1)}) custom-call(f32[1]{0:T(128)S(6)} %copy.19.gate_ref, bf16[1,128,8192]{2,1,0:T(8,128)(2,1)S(1)} %copy-done, s32[1,1024]{1,0:T(1,128)S(1)} %bitcast.14, ...), custom_call_target="tpu_custom_call", output_to_operand_aliasing={{0}: (5, {}), {1}: (6, {}), {2}: (7, {})} | custom-call | flops 805306368 | bytes 10485760 | tf_op jit(solution)/shard_map/attend/pallas_call | solution.py:106
  102.6 0.0 collective-permute-done.1.a_ref
  102.6 0.0 collective-permute-done.3.b_ref
  102.6 9.8 %attend.7 = bf16[1,128,8192]{2,1,0:T(8,128)(2,1)} custom-call(f32[1]{0:T(128)S(6)} %copy.19.gate_ref, bf16[1,128,8192]{2,1,0:T(8,128)(2,1)S(1)} %copy-done, s32[1,1024]{1,0:T(1,128)S(1)} %bitcast.15, bf16[6,2,16,1024]{3,2,1,0:T(8,128)(2,1)S(1)} %collective-permute-done.1.a_ref, bf16[6,2,16,1024]{3,2,1,0:T(8,128)(2,1)S(1)} %collective-permute-done.3.b_ref, ...), custom_call_target="tpu_custom_call" | custom-call | flops 805306368 | bytes 10485760 | tf_op jit(solution)/shard_map/attend/pallas_call | solution.py:106
  (1 shorter events, 0.0 us)
Async XLA Ops:
  52.3 14.7 %collective-permute-start = (bf16[6,2,16,1024]{3,2,1,0:T(8,128)(2,1)S(1)}, bf16[6,2,16,1024]{3,2,1,0:T(8,128)(2,1)S(1)}, u32[]{:S(2)}, u32[]{:S(2)}) collective-permute-start(bf16[6,2,16,1024]{3,2,1,0:T(8,128)(2,1)S(1)} %bitcast.6), channel_id=1, source_target_pairs={{0,12},{12,24},{24,36},{36,0},{1,13},{13,25},{25,37},{37,1},{2,14}... | collective-permute-start | bytes 1179656 | tf_op jit(solution)/shard_map/ppermute | solution.py:135
  55.7 13.9 %collective-permute-start.2 = (bf16[6,2,16,1024]{3,2,1,0:T(8,128)(2,1)S(1)}, bf16[6,2,16,1024]{3,2,1,0:T(8,128)(2,1)S(1)}, u32[]{:S(2)}, u32[]{:S(2)}) collective-permute-start(bf16[6,2,16,1024]{3,2,1,0:T(8,128)(2,1)S(1)} %bitcast.9), channel_id=1, source_target_pairs={{0,36},{12,0},{24,12},{36,24},{1,37},{13,1},{25,13},{37,25},{2,38}... | collective-permute-start | bytes 1179656 | tf_op jit(solution)/shard_map/ppermute | solution.py:136
  59.4 34.7 %collective-permute-start.4 = (bf16[6,2,16,1024]{3,2,1,0:T(8,128)(2,1)S(1)}, bf16[6,2,16,1024]{3,2,1,0:T(8,128)(2,1)S(1)}, u32[]{:S(2)}, u32[]{:S(2)}) collective-permute-start(bf16[6,2,16,1024]{3,2,1,0:T(8,128)(2,1)S(1)} %bitcast.10), channel_id=1, source_target_pairs={{0,12},{12,24},{24,36},{36,0},{1,13},{13,25},{25,37},{37,1},{2,14}... | collective-permute-start | bytes 1179656 | tf_op jit(solution)/shard_map/ppermute | solution.py:137
  61.6 32.5 %collective-permute-start.5 = (bf16[6,2,16,1024]{3,2,1,0:T(8,128)(2,1)S(1)}, bf16[6,2,16,1024]{3,2,1,0:T(8,128)(2,1)S(1)}, u32[]{:S(2)}, u32[]{:S(2)}) collective-permute-start(bf16[6,2,16,1024]{3,2,1,0:T(8,128)(2,1)S(1)} %bitcast.7), channel_id=1, source_target_pairs={{0,36},{12,0},{24,12},{36,24},{1,37},{13,1},{25,13},{37,25},{2,38}... | collective-permute-start | bytes 1179656 | tf_op jit(solution)/shard_map/ppermute | solution.py:138
  67.0 35.6 %collective-permute-start.1 = (bf16[6,2,16,1024]{3,2,1,0:T(8,128)(2,1)S(1)}, bf16[6,2,16,1024]{3,2,1,0:T(8,128)(2,1)S(1)}, u32[]{:S(2)}, u32[]{:S(2)}) collective-permute-start(bf16[6,2,16,1024]{3,2,1,0:T(8,128)(2,1)S(1)} %collective-permute-done.a_ref), channel_id=1, source_target_pairs={{0,12},{12,24},{24,36},{36,0},{1,13},{13,25},{25,37},{37,1},{2,14}... | collective-permute-start | bytes 1179656 | tf_op jit(solution)/shard_map/ppermute | solution.py:139
  69.6 33.1 %collective-permute-start.3 = (bf16[6,2,16,1024]{3,2,1,0:T(8,128)(2,1)S(1)}, bf16[6,2,16,1024]{3,2,1,0:T(8,128)(2,1)S(1)}, u32[]{:S(2)}, u32[]{:S(2)}) collective-permute-start(bf16[6,2,16,1024]{3,2,1,0:T(8,128)(2,1)S(1)} %collective-permute-done.2.b_ref), channel_id=1, source_target_pairs={{0,36},{12,0},{24,12},{36,24},{1,37},{13,1},{25,13},{37,25},{2,38}... | collective-permute-start | bytes 1179656 | tf_op jit(solution)/shard_map/ppermute | solution.py:140
  75.6 1.6 %copy-start = (bf16[1,128,8192]{2,1,0:T(8,128)(2,1)S(1)}, bf16[1,128,8192]{2,1,0:T(8,128)(2,1)}, u32[]{:S(2)}) copy-start(bf16[1,128,8192]{2,1,0:T(8,128)(2,1)} %q_ref.7) | copy-start | bytes 6291460

commit v2 on v1

v2 whole, which is shorter than its diff:
```python
import functools
import math

import jax
import jax.numpy as jnp
from jax import lax
from jax.experimental import pallas as pl
from jax.experimental.pallas import tpu as pltpu
from jax.sharding import Mesh, PartitionSpec as P

H = 64
KVH = 8
HD = 128
G = H // KVH
TILE = 192
NEG = -1e30

FINE = (("ylo", 4), ("core", 2), ("yhi", 2), ("x", 4), ("z", 12))
YRING = ("ylo", "core", "yhi")
LANES = 512
ONES = 16
VMEM_BYTES = 24 << 20


def attend_kernel(first, last, gate_ref, q_ref, seen_ref, bias_ref, a_ref, b_ref, *refs):
    old, refs = (None, refs) if first else (refs[:3], refs[3:])
    *refs, score_ref, weight_ref = refs
    factor = math.log2(math.e) / math.sqrt(HD)
    half = a_ref.shape[0] * a_ref.shape[2]
    count = a_ref.shape[2]
    total = 2 * half
    rows = q_ref.shape[1]
    heads = LANES // rows
    row = lax.broadcasted_iota(jnp.int32, (total, HD), 0)
    lane = lax.broadcasted_iota(jnp.int32, (total, HD), 1)
    chosen = (lane == row % count // (count // 4)).astype(jnp.bfloat16)
    ones = jnp.ones((ONES, total), jnp.bfloat16)

    def store(k):
        out_ref, made, sems = refs
        columns = pl.ds(pl.multiple_of(k * G * HD, G * HD), G * HD)
        return pltpu.make_async_copy(made.at[:, columns], out_ref.at[0, :, columns], sems.at[k])

    def columns_of(k):
        return pl.ds(pl.multiple_of(k * HD, HD), HD)

    def wide(k, c, g):
        return pl.ds(pl.multiple_of(k * G * HD + (c * heads + g) * HD, HD), HD)

    def both(k, which):
        columns = columns_of(k)
        return jnp.concatenate(
            [a_ref[:, which, :, columns].reshape(half, HD), b_ref[:, which, :, columns].reshape(half, HD)], axis=0
        )

    def scores(k, c):
        query = jnp.concatenate(
            [jnp.concatenate([q_ref[0, :, wide(k, c, g)], bias_ref[...]], axis=1) for g in range(heads)], axis=0
        )
        keys = jnp.concatenate([both(k, 0), chosen], axis=1)
        score = lax.dot_general(keys, query, (((1,), (1,)), ((), ())), preferred_element_type=jnp.float32)
        score = score.reshape(total // 8, 8, LANES)
        score_ref[c % 2] = score
        return jnp.max(score, axis=0)

    def finish(k, c, top, vals):
        lanes = slice(c * LANES, (c + 1) * LANES)
        top = jnp.max(top, axis=0, keepdims=True)
        new = top if first else jnp.maximum(top, old[0][k, :, lanes])
        expo = jnp.exp2((score_ref[c % 2] - new) * factor)
        weight_ref[c % 2] = expo.astype(jnp.bfloat16).reshape(total, LANES)
        summed = jnp.dot(vals, weight_ref[c % 2], preferred_element_type=jnp.float32)
        acc, denom = summed[:HD], summed[HD : HD + 1]
        if not first:
            scale = jnp.exp2((old[0][k, :, lanes] - new) * factor)
            denom = denom + old[1][k, :, lanes] * scale
            acc = acc + old[2][k, :, lanes] * scale
        if last:
            ratio = jnp.where(seen_ref[:, lanes] > 0, jnp.tanh(gate_ref[0]) / denom, 0.0)
            result = acc * ratio
            for g in range(heads):
                piece = result[:, g * rows : (g + 1) * rows].T
                refs[1][:, wide(k, c, g)] = piece.astype(jnp.bfloat16)
        else:
            refs[0][k, :, lanes] = new
            refs[1][k, :, lanes] = denom
            refs[2][k, :, lanes] = acc

    chunks = G * rows // LANES

    def head(k, top):
        vals = jnp.concatenate([both(k, 1).T, ones], axis=0)
        for c in range(chunks):
            ahead = scores(k, c + 1) if c + 1 < chunks else scores(jnp.minimum(k + 1, KVH - 1), 0)
            finish(k, c, top, vals)
            top = ahead
        if last:
            store(k).start()
        return top

    lax.fori_loop(0, KVH, head, scores(0, 0), unroll=2)
    if last:
        lax.fori_loop(0, KVH, lambda k, carry: (store(k).wait(), carry)[1], 0)


def attend(gate, queries, seen, bias, halves, state, last):
    rows = queries.shape[1]
    lanes = G * rows
    steps, _, count, _ = halves[0].shape
    first = state is None
    vmem = pl.BlockSpec(memory_space=pltpu.VMEM)
    operands = [gate, queries, seen, bias, *halves]
    in_specs = [pl.BlockSpec(memory_space=pltpu.SMEM)] + [vmem] * 5
    aliases = {}
    total = 2 * steps * count
    buffers = [
        pltpu.VMEM((2, total // 8, 8, LANES), jnp.float32),
        pltpu.VMEM((2, total, LANES), jnp.bfloat16),
    ]
    scratch = []
    if not first:
        if not last:
            aliases = {len(operands) + i: i for i in range(3)}
        in_specs += [vmem] * 3
        operands += list(state)
    if last:
        out_shape = jax.ShapeDtypeStruct(queries.shape, jnp.bfloat16)
        out_specs = pl.BlockSpec(memory_space=pl.ANY)
        scratch = [pltpu.VMEM((rows, H * HD), jnp.bfloat16), pltpu.SemaphoreType.DMA((KVH,))]
    else:
        stat = jax.ShapeDtypeStruct((KVH, 1, lanes), jnp.float32)
        out_shape = [stat, stat, jax.ShapeDtypeStruct((KVH, HD, lanes), jnp.float32)]
        out_specs = [vmem] * 3
    return pl.pallas_call(
        functools.partial(attend_kernel, first, last),
        in_specs=in_specs,
        out_specs=out_specs,
        out_shape=out_shape,
        scratch_shapes=scratch + buffers,
        input_output_aliases=aliases,
        name="attend",
        compiler_params=pltpu.CompilerParams(vmem_limit_bytes=VMEM_BYTES),
        cost_estimate=pl.CostEstimate(
            flops=4 * H * rows * total * HD,
            bytes_accessed=2 * H * rows * HD + 8 * H * rows * HD,
            transcendentals=H * rows * total,
        ),
    )(*operands)


def body(queries, image_kv, visible, gate):
    layers = image_kv.shape[0]
    ring = lax.axis_size("x")
    seen = jnp.tile(visible, G)[None]
    starts = jnp.arange(HD, dtype=jnp.int32) * TILE
    bias = jnp.where(starts < visible[:, None], 0.0, NEG).astype(jnp.bfloat16)
    sent = jnp.repeat(image_kv[:, :, 0], lax.axis_size("yhi"), axis=0)
    mine = lax.all_to_all(sent, YRING, split_axis=0, concat_axis=0, tiled=True)
    mine = jnp.transpose(mine, (1, 0, 2))
    own = lax.all_gather(mine, "z")
    middle = own.shape[0] // 2
    low, high = own[:middle], own[middle:]
    up = [(i, (i + 1) % ring) for i in range(ring)]
    down = [(i, (i - 1) % ring) for i in range(ring)]
    low_left = lax.ppermute(low, "x", up)
    high_right = lax.ppermute(high, "x", down)
    high_left = lax.ppermute(high, "x", up)
    low_right = lax.ppermute(low, "x", down)
    low_far = lax.ppermute(low_left, "x", up)
    high_far = lax.ppermute(high_right, "x", down)
    state = attend(gate, queries, seen, bias, (low, high), None, False)
    state = attend(gate, queries, seen, bias, (low_left, high_right), state, False)
    state = attend(gate, queries, seen, bias, (high_left, low_right), state, False)
    return attend(gate, queries, seen, bias, (low_far, high_far), state, True)


def solution(mesh):
    fine = Mesh(mesh.devices.reshape([n for _, n in FINE]), [a for a, _ in FINE])
    section, dp = ("ylo", "core"), ("yhi", "x", "z")
    in_specs = (
        P(section, dp, None),
        P(None, None, section + dp, None),
        P(dp),
        P(section),
    )
    return jax.shard_map(body, mesh=fine, in_specs=in_specs, out_specs=P(section, dp, None), check_vma=False)
```

time: 113 us -> 94.8 us (0.84)
  Pallas kernels: 35.1 us -> 17 us
    pallas_call x4, Pallas kernels: 35.1 us -> 17 us  [attend(): pl.pallas_call(functools.partial(attend_kernel, first, last), in_specs=in...]
  transfers between devices with their start and end apart: 6 -> 6, of which waited for: 1 -> 0; matrix products, arithmetic and copies ran while one was open for 1% -> 1% of each run, Pallas kernels for 23% -> 12%
where the time goes in v2:
time: 94.8 us; the launch traced here: 94.4 us
  blocking collectives  51.4 us (54%)
  starting transfers between devices  21.3 us (22%)
  Pallas kernels  17 us (18%)
  local copies, waits for them, and re-layouts  3.12 us (3%)
    all_gather x1, blocking collectives, body(): own = lax.all_gather(mine, 'z')  32.5 us
    all_to_all x1, blocking collectives, body(): mine = lax.all_to_all(sent, YRING, split_axis=0, concat_axis=0, tiled=True)  18.9 us
    pallas_call x4, Pallas kernels, attend(): pl.pallas_call(functools.partial(attend_kernel, first, last), in_specs=in...  17 us
    ppermute x1, starting transfers between devices, body(): low_right = lax.ppermute(low, 'x', down)  4.86 us
    ppermute x1, starting transfers between devices, body(): high_far = lax.ppermute(high_right, 'x', down)  4.73 us
    ppermute x1, starting transfers between devices, body(): high_right = lax.ppermute(high, 'x', down)  3.65 us
    ppermute x1, starting transfers between devices, body(): low_left = lax.ppermute(low, 'x', up)  3.4 us
    ppermute x1, starting transfers between devices, body(): low_far = lax.ppermute(low_left, 'x', up)  2.46 us
  transfers between devices with their start and end apart: 6, of which 0 were waited for; matrix products, arithmetic and copies ran while one was open for 1% of the time, Pallas kernels for 12%

profile of v2, /device:TPU:8, one launch (start us, length us, event | category | flops | bytes accessed | tf_op | source)
XLA Modules:
  0.0 94.4 jit_solution(4131275547353183876)
XLA Ops:
  0.0 0.8 broadcast_in_dim.15
  0.8 18.9 %all_to_all.5 = bf16[16,2,1024]{2,1,0:T(2,128)(2,1)S(1)} all-to-all(bf16[16,2,1024]{2,1,0:T(2,128)(2,1)S(1)} %bitcast.17), channel_id=1, replica_groups=mesh['ylo'=4,'core'=2,'yhi'=2,'x'=4,'z'=12] {'ylo','core','yhi'}, dimensions={0} | all-to-all | bytes 131072 | tf_op jit(solution)/shard_map/all_to_all | solution.py:158
  19.7 32.5 %all-gather = bf16[24,16,1024]{2,1,0:T(8,128)(2,1)S(1)} all-gather(bf16[2,16,1024]{2,1,0:T(8,128)(2,1)S(1)} %copy.12), channel_id=2, replica_groups=mesh['ylo'=4,'core'=2,'yhi'=2,'x'=4,'z'=12] {'z'}, dimensions={0}, use_global_device_ids=true | all-gather | bytes 851968 | tf_op jit(solution)/shard_map/all_gather | solution.py:160
  52.2 0.1 fusion
  52.3 3.4 %collective-permute-start = (bf16[6,2,16,1024]{3,2,1,0:T(8,128)(2,1)S(1)}, bf16[6,2,16,1024]{3,2,1,0:T(8,128)(2,1)S(1)}, u32[]{:S(2)}, u32[]{:S(2)}) collective-permute-start(bf16[6,2,16,1024]{3,2,1,0:T(8,128)(2,1)S(1)} %bitcast.6), channel_id=1, source_target_pairs={{0,12},{12,24},{24,36},{36,0},{1,13},{13,25},{25,37},{37,1},{2,14}... | collective-permute-start | bytes 1179656 | tf_op jit(solution)/shard_map/ppermute | solution.py:165
  55.7 3.7 %collective-permute-start.2 = (bf16[6,2,16,1024]{3,2,1,0:T(8,128)(2,1)S(1)}, bf16[6,2,16,1024]{3,2,1,0:T(8,128)(2,1)S(1)}, u32[]{:S(2)}, u32[]{:S(2)}) collective-permute-start(bf16[6,2,16,1024]{3,2,1,0:T(8,128)(2,1)S(1)} %bitcast.9), channel_id=1, source_target_pairs={{0,36},{12,0},{24,12},{36,24},{1,37},{13,1},{25,13},{37,25},{2,38}... | collective-permute-start | bytes 1179656 | tf_op jit(solution)/shard_map/ppermute | solution.py:166
  59.4 2.2 %collective-permute-start.4 = (bf16[6,2,16,1024]{3,2,1,0:T(8,128)(2,1)S(1)}, bf16[6,2,16,1024]{3,2,1,0:T(8,128)(2,1)S(1)}, u32[]{:S(2)}, u32[]{:S(2)}) collective-permute-start(bf16[6,2,16,1024]{3,2,1,0:T(8,128)(2,1)S(1)} %bitcast.10), channel_id=1, source_target_pairs={{0,12},{12,24},{24,36},{36,0},{1,13},{13,25},{25,37},{37,1},{2,14}... | collective-permute-start | bytes 1179656 | tf_op jit(solution)/shard_map/ppermute | solution.py:167
  61.6 4.9 %collective-permute-start.5 = (bf16[6,2,16,1024]{3,2,1,0:T(8,128)(2,1)S(1)}, bf16[6,2,16,1024]{3,2,1,0:T(8,128)(2,1)S(1)}, u32[]{:S(2)}, u32[]{:S(2)}) collective-permute-start(bf16[6,2,16,1024]{3,2,1,0:T(8,128)(2,1)S(1)} %bitcast.7), channel_id=1, source_target_pairs={{0,36},{12,0},{24,12},{36,24},{1,37},{13,1},{25,13},{37,25},{2,38}... | collective-permute-start | bytes 1179656 | tf_op jit(solution)/shard_map/ppermute | solution.py:168
  67.1 0.0 collective-permute-done.a_ref
  67.1 2.5 %collective-permute-start.1 = (bf16[6,2,16,1024]{3,2,1,0:T(8,128)(2,1)S(1)}, bf16[6,2,16,1024]{3,2,1,0:T(8,128)(2,1)S(1)}, u32[]{:S(2)}, u32[]{:S(2)}) collective-permute-start(bf16[6,2,16,1024]{3,2,1,0:T(8,128)(2,1)S(1)} %collective-permute-done.a_ref), channel_id=1, source_target_pairs={{0,12},{12,24},{24,36},{36,0},{1,13},{13,25},{25,37},{37,1},{2,14}... | collective-permute-start | bytes 1179656 | tf_op jit(solution)/shard_map/ppermute | solution.py:169
  69.6 0.0 collective-permute-done.2.b_ref
  69.6 4.7 %collective-permute-start.3 = (bf16[6,2,16,1024]{3,2,1,0:T(8,128)(2,1)S(1)}, bf16[6,2,16,1024]{3,2,1,0:T(8,128)(2,1)S(1)}, u32[]{:S(2)}, u32[]{:S(2)}) collective-permute-start(bf16[6,2,16,1024]{3,2,1,0:T(8,128)(2,1)S(1)} %collective-permute-done.2.b_ref), channel_id=1, source_target_pairs={{0,36},{12,0},{24,12},{36,24},{1,37},{13,1},{25,13},{37,25},{2,38}... | collective-permute-start | bytes 1179656 | tf_op jit(solution)/shard_map/ppermute | solution.py:170
  74.3 0.7 select_convert_fusion.bias_ref
  75.1 0.7 tile.2
  75.7 0.0 copy-start
  75.7 1.6 %copy-done = bf16[1,128,8192]{2,1,0:T(8,128)(2,1)S(1)} copy-done((bf16[1,128,8192]{2,1,0:T(8,128)(2,1)S(1)}, bf16[1,128,8192]{2,1,0:T(8,128)(2,1)}, u32[]{:S(2)}) %copy-start) | copy-done | bytes 2097176
  77.3 3.8 %attend.4 = (f32[8,1,1024]{2,1,0:T(1,128)S(1)}, f32[8,1,1024]{2,1,0:T(1,128)S(1)}, f32[8,128,1024]{2,1,0:T(8,128)S(1)}) custom-call(f32[1]{0:T(128)S(6)} %copy.19.gate_ref, bf16[1,128,8192]{2,1,0:T(8,128)(2,1)S(1)} %copy-done, s32[1,1024]{1,0:T(1,128)S(1)} %bitcast.12, bf16[128,128]{1,0:T(8,128)(2,1)S(1)} %select_convert_fusion.bias_ref, ...), custom_call_target="tpu_custom_call" | custom-call | flops 805306368 | bytes 10485760 | tf_op jit(solution)/shard_map/attend/pallas_call | solution.py:134
  81.1 3.9 %attend.5 = (f32[8,1,1024]{2,1,0:T(1,128)S(1)}, f32[8,1,1024]{2,1,0:T(1,128)S(1)}, f32[8,128,1024]{2,1,0:T(8,128)S(1)}) custom-call(f32[1]{0:T(128)S(6)} %copy.19.gate_ref, bf16[1,128,8192]{2,1,0:T(8,128)(2,1)S(1)} %copy-done, s32[1,1024]{1,0:T(1,128)S(1)} %bitcast.13, ...), custom_call_target="tpu_custom_call", output_to_operand_aliasing={{0}: (6, {}), {1}: (7, {}), {2}: (8, {})} | custom-call | flops 805306368 | bytes 10485760 | tf_op jit(solution)/shard_map/attend/pallas_call | solution.py:134
  85.1 0.0 collective-permute-done.4.a_ref
  85.1 0.0 collective-permute-done.5.b_ref
  85.1 3.9 %attend.6 = (f32[8,1,1024]{2,1,0:T(1,128)S(1)}, f32[8,1,1024]{2,1,0:T(1,128)S(1)}, f32[8,128,1024]{2,1,0:T(8,128)S(1)}) custom-call(f32[1]{0:T(128)S(6)} %copy.19.gate_ref, bf16[1,128,8192]{2,1,0:T(8,128)(2,1)S(1)} %copy-done, s32[1,1024]{1,0:T(1,128)S(1)} %bitcast.14, ...), custom_call_target="tpu_custom_call", output_to_operand_aliasing={{0}: (6, {}), {1}: (7, {}), {2}: (8, {})} | custom-call | flops 805306368 | bytes 10485760 | tf_op jit(solution)/shard_map/attend/pallas_call | solution.py:134
  89.0 0.0 collective-permute-done.1.a_ref
  89.0 0.0 collective-permute-done.3.b_ref
  89.0 5.3 %attend.7 = bf16[1,128,8192]{2,1,0:T(8,128)(2,1)} custom-call(f32[1]{0:T(128)S(6)} %copy.19.gate_ref, bf16[1,128,8192]{2,1,0:T(8,128)(2,1)S(1)} %copy-done, s32[1,1024]{1,0:T(1,128)S(1)} %bitcast.15, bf16[128,128]{1,0:T(8,128)(2,1)S(1)} %select_convert_fusion.bias_ref, bf16[6,2,16,1024]{3,2,1,0:T(8,128)(2,1)S(1)} %collective-permute-done.1.a_ref, ...), custom_call_target="tpu_custom_call" | custom-call | flops 805306368 | bytes 10485760 | tf_op jit(solution)/shard_map/attend/pallas_call | solution.py:134
  (2 shorter events, 0.0 us)
Async XLA Ops:
  52.3 14.8 %collective-permute-start = (bf16[6,2,16,1024]{3,2,1,0:T(8,128)(2,1)S(1)}, bf16[6,2,16,1024]{3,2,1,0:T(8,128)(2,1)S(1)}, u32[]{:S(2)}, u32[]{:S(2)}) collective-permute-start(bf16[6,2,16,1024]{3,2,1,0:T(8,128)(2,1)S(1)} %bitcast.6), channel_id=1, source_target_pairs={{0,12},{12,24},{24,36},{36,0},{1,13},{13,25},{25,37},{37,1},{2,14}... | collective-permute-start | bytes 1179656 | tf_op jit(solution)/shard_map/ppermute | solution.py:165
  55.7 13.9 %collective-permute-start.2 = (bf16[6,2,16,1024]{3,2,1,0:T(8,128)(2,1)S(1)}, bf16[6,2,16,1024]{3,2,1,0:T(8,128)(2,1)S(1)}, u32[]{:S(2)}, u32[]{:S(2)}) collective-permute-start(bf16[6,2,16,1024]{3,2,1,0:T(8,128)(2,1)S(1)} %bitcast.9), channel_id=1, source_target_pairs={{0,36},{12,0},{24,12},{36,24},{1,37},{13,1},{25,13},{37,25},{2,38}... | collective-permute-start | bytes 1179656 | tf_op jit(solution)/shard_map/ppermute | solution.py:166
  59.4 25.7 %collective-permute-start.4 = (bf16[6,2,16,1024]{3,2,1,0:T(8,128)(2,1)S(1)}, bf16[6,2,16,1024]{3,2,1,0:T(8,128)(2,1)S(1)}, u32[]{:S(2)}, u32[]{:S(2)}) collective-permute-start(bf16[6,2,16,1024]{3,2,1,0:T(8,128)(2,1)S(1)} %bitcast.10), channel_id=1, source_target_pairs={{0,12},{12,24},{24,36},{36,0},{1,13},{13,25},{25,37},{37,1},{2,14}... | collective-permute-start | bytes 1179656 | tf_op jit(solution)/shard_map/ppermute | solution.py:167
  61.6 23.5 %collective-permute-start.5 = (bf16[6,2,16,1024]{3,2,1,0:T(8,128)(2,1)S(1)}, bf16[6,2,16,1024]{3,2,1,0:T(8,128)(2,1)S(1)}, u32[]{:S(2)}, u32[]{:S(2)}) collective-permute-start(bf16[6,2,16,1024]{3,2,1,0:T(8,128)(2,1)S(1)} %bitcast.7), channel_id=1, source_target_pairs={{0,36},{12,0},{24,12},{36,24},{1,37},{13,1},{25,13},{37,25},{2,38}... | collective-permute-start | bytes 1179656 | tf_op jit(solution)/shard_map/ppermute | solution.py:168
  67.1 21.9 %collective-permute-start.1 = (bf16[6,2,16,1024]{3,2,1,0:T(8,128)(2,1)S(1)}, bf16[6,2,16,1024]{3,2,1,0:T(8,128)(2,1)S(1)}, u32[]{:S(2)}, u32[]{:S(2)}) collective-permute-start(bf16[6,2,16,1024]{3,2,1,0:T(8,128)(2,1)S(1)} %collective-permute-done.a_ref), channel_id=1, source_target_pairs={{0,12},{12,24},{24,36},{36,0},{1,13},{13,25},{25,37},{37,1},{2,14}... | collective-permute-start | bytes 1179656 | tf_op jit(solution)/shard_map/ppermute | solution.py:169
  69.6 19.4 %collective-permute-start.3 = (bf16[6,2,16,1024]{3,2,1,0:T(8,128)(2,1)S(1)}, bf16[6,2,16,1024]{3,2,1,0:T(8,128)(2,1)S(1)}, u32[]{:S(2)}, u32[]{:S(2)}) collective-permute-start(bf16[6,2,16,1024]{3,2,1,0:T(8,128)(2,1)S(1)} %collective-permute-done.2.b_ref), channel_id=1, source_target_pairs={{0,36},{12,0},{24,12},{36,24},{1,37},{13,1},{25,13},{37,25},{2,38}... | collective-permute-start | bytes 1179656 | tf_op jit(solution)/shard_map/ppermute | solution.py:170
  75.7 1.6 %copy-start = (bf16[1,128,8192]{2,1,0:T(8,128)(2,1)S(1)}, bf16[1,128,8192]{2,1,0:T(8,128)(2,1)}, u32[]{:S(2)}) copy-start(bf16[1,128,8192]{2,1,0:T(8,128)(2,1)} %q_ref.7) | copy-start | bytes 6291460

commit v3 on v2

--- a/solution.py
+++ b/solution.py
@@ -22,42 +22,44 @@
 VMEM_BYTES = 24 << 20
 
 
-def attend_kernel(first, last, gate_ref, q_ref, seen_ref, bias_ref, a_ref, b_ref, *refs):
+def attend_kernel(first, last, parts, gate_ref, q_ref, seen_ref, *refs):
+    part_refs, refs = refs[:parts], refs[parts:]
     old, refs = (None, refs) if first else (refs[:3], refs[3:])
     *refs, score_ref, weight_ref = refs
     factor = math.log2(math.e) / math.sqrt(HD)
-    half = a_ref.shape[0] * a_ref.shape[2]
-    count = a_ref.shape[2]
-    total = 2 * half
+    count = part_refs[0].shape[2]
+    sizes = [p.shape[0] * count for p in part_refs]
+    total = sum(sizes)
     rows = q_ref.shape[1]
     heads = LANES // rows
+    reach = jnp.broadcast_to(seen_ref[...].astype(jnp.float32), (HD, rows)).T
+    starts = (lax.broadcasted_iota(jnp.int32, (rows, HD), 1) * TILE).astype(jnp.float32)
+    bias = jnp.where(starts < reach, 0.0, NEG).astype(jnp.bfloat16)
     row = lax.broadcasted_iota(jnp.int32, (total, HD), 0)
     lane = lax.broadcasted_iota(jnp.int32, (total, HD), 1)
     chosen = (lane == row % count // (count // 4)).astype(jnp.bfloat16)
     ones = jnp.ones((ONES, total), jnp.bfloat16)
+    seen = jnp.concatenate([seen_ref[...]] * heads, axis=1)
 
     def store(k):
         out_ref, made, sems = refs
         columns = pl.ds(pl.multiple_of(k * G * HD, G * HD), G * HD)
         return pltpu.make_async_copy(made.at[:, columns], out_ref.at[0, :, columns], sems.at[k])
 
-    def columns_of(k):
-        return pl.ds(pl.multiple_of(k * HD, HD), HD)
-
     def wide(k, c, g):
         return pl.ds(pl.multiple_of(k * G * HD + (c * heads + g) * HD, HD), HD)
 
-    def both(k, which):
-        columns = columns_of(k)
+    def gather(k, which):
+        columns = pl.ds(pl.multiple_of(k * HD, HD), HD)
         return jnp.concatenate(
-            [a_ref[:, which, :, columns].reshape(half, HD), b_ref[:, which, :, columns].reshape(half, HD)], axis=0
+            [p[:, which, :, columns].reshape(n, HD) for p, n in zip(part_refs, sizes)], axis=0
         )
 
     def scores(k, c):
         query = jnp.concatenate(
-            [jnp.concatenate([q_ref[0, :, wide(k, c, g)], bias_ref[...]], axis=1) for g in range(heads)], axis=0
+            [jnp.concatenate([q_ref[0, :, wide(k, c, g)], bias], axis=1) for g in range(heads)], axis=0
         )
-        keys = jnp.concatenate([both(k, 0), chosen], axis=1)
+        keys = jnp.concatenate([gather(k, 0), chosen], axis=1)
         score = lax.dot_general(keys, query, (((1,), (1,)), ((), ())), preferred_element_type=jnp.float32)
         score = score.reshape(total // 8, 8, LANES)
         score_ref[c % 2] = score
@@ -76,11 +78,10 @@
             denom = denom + old[1][k, :, lanes] * scale
             acc = acc + old[2][k, :, lanes] * scale
         if last:
-            ratio = jnp.where(seen_ref[:, lanes] > 0, jnp.tanh(gate_ref[0]) / denom, 0.0)
-            result = acc * ratio
+            ratio = jnp.where(seen > 0, jnp.tanh(gate_ref[0]) / denom, 0.0)
+            result = (acc * ratio).astype(jnp.bfloat16)
             for g in range(heads):
-                piece = result[:, g * rows : (g + 1) * rows].T
-                refs[1][:, wide(k, c, g)] = piece.astype(jnp.bfloat16)
+                refs[1][:, wide(k, c, g)] = result[:, g * rows : (g + 1) * rows].T
         else:
             refs[0][k, :, lanes] = new
             refs[1][k, :, lanes] = denom
@@ -89,30 +90,33 @@
     chunks = G * rows // LANES
 
     def head(k, top):
-        vals = jnp.concatenate([both(k, 1).T, ones], axis=0)
+        vals = jnp.concatenate([gather(k, 1).T, ones], axis=0)
         for c in range(chunks):
-            ahead = scores(k, c + 1) if c + 1 < chunks else scores(jnp.minimum(k + 1, KVH - 1), 0)
+            if c + 1 < chunks:
+                ahead = scores(k, c + 1)
+            else:
+                ahead = scores(jnp.minimum(k + 1, KVH - 1), 0)
             finish(k, c, top, vals)
             top = ahead
         if last:
             store(k).start()
         return top
 
-    lax.fori_loop(0, KVH, head, scores(0, 0), unroll=2)
+    lax.fori_loop(0, KVH, head, scores(0, 0), unroll=4)
     if last:
         lax.fori_loop(0, KVH, lambda k, carry: (store(k).wait(), carry)[1], 0)
 
 
-def attend(gate, queries, seen, bias, halves, state, last):
+def attend(gate, queries, seen, parts, state, last):
     rows = queries.shape[1]
     lanes = G * rows
-    steps, _, count, _ = halves[0].shape
+    count = parts[0].shape[2]
     first = state is None
     vmem = pl.BlockSpec(memory_space=pltpu.VMEM)
-    operands = [gate, queries, seen, bias, *halves]
-    in_specs = [pl.BlockSpec(memory_space=pltpu.SMEM)] + [vmem] * 5
+    operands = [gate, queries, seen, *parts]
+    in_specs = [pl.BlockSpec(memory_space=pltpu.SMEM)] + [vmem] * (2 + len(parts))
     aliases = {}
-    total = 2 * steps * count
+    total = sum(p.shape[0] * count for p in parts)
     buffers = [
         pltpu.VMEM((2, total // 8, 8, LANES), jnp.float32),
         pltpu.VMEM((2, total, LANES), jnp.bfloat16),
@@ -130,9 +134,9 @@
     else:
         stat = jax.ShapeDtypeStruct((KVH, 1, lanes), jnp.float32)
         out_shape = [stat, stat, jax.ShapeDtypeStruct((KVH, HD, lanes), jnp.float32)]
-        out_specs = [vmem] * 3
+        out_specs = [vmem] * len(out_shape)
     return pl.pallas_call(
-        functools.partial(attend_kernel, first, last),
+        functools.partial(attend_kernel, first, last, len(parts)),
         in_specs=in_specs,
         out_specs=out_specs,
         out_shape=out_shape,
@@ -149,11 +153,8 @@
 
 
 def body(queries, image_kv, visible, gate):
-    layers = image_kv.shape[0]
     ring = lax.axis_size("x")
-    seen = jnp.tile(visible, G)[None]
-    starts = jnp.arange(HD, dtype=jnp.int32) * TILE
-    bias = jnp.where(starts < visible[:, None], 0.0, NEG).astype(jnp.bfloat16)
+    seen = visible[None]
     sent = jnp.repeat(image_kv[:, :, 0], lax.axis_size("yhi"), axis=0)
     mine = lax.all_to_all(sent, YRING, split_axis=0, concat_axis=0, tiled=True)
     mine = jnp.transpose(mine, (1, 0, 2))
@@ -168,10 +169,8 @@
     low_right = lax.ppermute(low, "x", down)
     low_far = lax.ppermute(low_left, "x", up)
     high_far = lax.ppermute(high_right, "x", down)
-    state = attend(gate, queries, seen, bias, (low, high), None, False)
-    state = attend(gate, queries, seen, bias, (low_left, high_right), state, False)
-    state = attend(gate, queries, seen, bias, (high_left, low_right), state, False)
-    return attend(gate, queries, seen, bias, (low_far, high_far), state, True)
+    state = attend(gate, queries, seen, (low, high, low_left, high_right), None, False)
+    return attend(gate, queries, seen, (high_left, low_right, low_far, high_far), state, True)
 
 
 def solution(mesh):

time: 94.8 us -> 89.4 us (0.943)
  Pallas kernels: 17 us -> 11.2 us
  waiting for transfers between devices: 0.02 us -> 5.19 us
  local copies, waits for them, and re-layouts: 3.12 us -> 1.03 us
  starting transfers between devices: 21.3 us -> 19.5 us
    pallas_call x4 -> x2, Pallas kernels: 17 us -> 11.2 us  [attend(): pl.pallas_call(functools.partial(attend_kernel, first, last, len(parts)),...]
    ppermute x1, waiting for transfers between devices: 0.01 us -> 3.44 us  [body(): low_far = lax.ppermute(low_left, 'x', up)]
    unnamed x2 -> x4, local copies, waits for them, and re-layouts: 1.59 us -> 0.01 us
    ppermute x1, starting transfers between devices: 3.4 us -> 1.92 us  [body(): low_left = lax.ppermute(low, 'x', up)]
    ppermute x1, starting transfers between devices: 3.65 us -> 4.67 us  [body(): high_right = lax.ppermute(high, 'x', down)]
  transfers between devices with their start and end apart: 6 -> 6, of which waited for: 0 -> 4; matrix products, arithmetic and copies ran while one was open for 1% -> 0% of each run, Pallas kernels for 12% -> 5%
where the time goes in v3:
time: 89.4 us; the launch traced here: 89 us
  blocking collectives  51.4 us (57%)
  starting transfers between devices  19.5 us (22%)
  Pallas kernels  11.2 us (13%)
  waiting for transfers between devices  5.19 us (6%)
  local copies, waits for them, and re-layouts  1.03 us (1%)
    all_gather x1, blocking collectives, body(): own = lax.all_gather(mine, 'z')  32.5 us
    all_to_all x1, blocking collectives, body(): mine = lax.all_to_all(sent, YRING, split_axis=0, concat_axis=0, tiled=True)  18.9 us
    pallas_call x2, Pallas kernels, attend(): pl.pallas_call(functools.partial(attend_kernel, first, last, len(parts)),...  11.2 us
    ppermute x1, starting transfers between devices, body(): high_right = lax.ppermute(high, 'x', down)  4.67 us
    ppermute x1, starting transfers between devices, body(): low_right = lax.ppermute(low, 'x', down)  4.4 us
    ppermute x1, starting transfers between devices, body(): high_far = lax.ppermute(high_right, 'x', down)  3.92 us
    ppermute x1, waiting for transfers between devices, body(): low_far = lax.ppermute(low_left, 'x', up)  3.44 us
    ppermute x1, starting transfers between devices, body(): high_left = lax.ppermute(high, 'x', up)  2.65 us
  transfers between devices with their start and end apart: 6, of which 4 were waited for; matrix products, arithmetic and copies ran while one was open for 0% of the time, Pallas kernels for 5%

profile of v3, /device:TPU:8, one launch (start us, length us, event | category | flops | bytes accessed | tf_op | source)
XLA Modules:
  0.0 89.0 jit_solution(14431972853888540725)
XLA Ops:
  0.0 0.0 copy-start
  0.0 0.0 copy-start.1
  0.0 0.9 %broadcast_in_dim.7 = bf16[8,2,2,1024]{3,2,1,0:T(2,128)(2,1)S(1)} broadcast(bf16[8,2,1024]{2,1,0:T(2,128)(2,1)} %bitcast.16), dimensions={0,2,3} | broadcast | bytes 98304 | tf_op jit(solution)/shard_map/broadcast_in_dim | solution.py:158
  1.0 18.9 %all_to_all.5 = bf16[16,2,1024]{2,1,0:T(2,128)(2,1)S(1)} all-to-all(bf16[16,2,1024]{2,1,0:T(2,128)(2,1)S(1)} %bitcast.15), channel_id=1, replica_groups=mesh['ylo'=4,'core'=2,'yhi'=2,'x'=4,'z'=12] {'ylo','core','yhi'}, dimensions={0} | all-to-all | bytes 131072 | tf_op jit(solution)/shard_map/all_to_all | solution.py:159
  19.9 32.5 %all-gather = bf16[24,16,1024]{2,1,0:T(8,128)(2,1)S(1)} all-gather(bf16[2,16,1024]{2,1,0:T(8,128)(2,1)S(1)} %copy.6), channel_id=2, replica_groups=mesh['ylo'=4,'core'=2,'yhi'=2,'x'=4,'z'=12] {'z'}, dimensions={0}, use_global_device_ids=true | all-gather | bytes 851968 | tf_op jit(solution)/shard_map/all_gather | solution.py:161
  52.4 0.1 fusion
  52.5 4.7 %collective-permute-start.4 = (bf16[6,2,16,1024]{3,2,1,0:T(8,128)(2,1)S(1)}, bf16[6,2,16,1024]{3,2,1,0:T(8,128)(2,1)S(1)}, u32[]{:S(2)}, u32[]{:S(2)}) collective-permute-start(bf16[6,2,16,1024]{3,2,1,0:T(8,128)(2,1)S(1)} %bitcast.9), channel_id=1, source_target_pairs={{0,36},{12,0},{24,12},{36,24},{1,37},{13,1},{25,13},{37,25},{2,38}... | collective-permute-start | bytes 1179656 | tf_op jit(solution)/shard_map/ppermute | solution.py:167
  57.1 1.9 %collective-permute-start.2 = (bf16[6,2,16,1024]{3,2,1,0:T(8,128)(2,1)S(1)}, bf16[6,2,16,1024]{3,2,1,0:T(8,128)(2,1)S(1)}, u32[]{:S(2)}, u32[]{:S(2)}) collective-permute-start(bf16[6,2,16,1024]{3,2,1,0:T(8,128)(2,1)S(1)} %bitcast.6), channel_id=1, source_target_pairs={{0,12},{12,24},{24,36},{36,0},{1,13},{13,25},{25,37},{37,1},{2,14}... | collective-permute-start | bytes 1179656 | tf_op jit(solution)/shard_map/ppermute | solution.py:166
  59.1 2.7 %collective-permute-start = (bf16[6,2,16,1024]{3,2,1,0:T(8,128)(2,1)S(1)}, bf16[6,2,16,1024]{3,2,1,0:T(8,128)(2,1)S(1)}, u32[]{:S(2)}, u32[]{:S(2)}) collective-permute-start(bf16[6,2,16,1024]{3,2,1,0:T(8,128)(2,1)S(1)} %bitcast.10), channel_id=1, source_target_pairs={{0,12},{12,24},{24,36},{36,0},{1,13},{13,25},{25,37},{37,1},{2,14}... | collective-permute-start | bytes 1179656 | tf_op jit(solution)/shard_map/ppermute | solution.py:168
  61.7 4.4 %collective-permute-start.1 = (bf16[6,2,16,1024]{3,2,1,0:T(8,128)(2,1)S(1)}, bf16[6,2,16,1024]{3,2,1,0:T(8,128)(2,1)S(1)}, u32[]{:S(2)}, u32[]{:S(2)}) collective-permute-start(bf16[6,2,16,1024]{3,2,1,0:T(8,128)(2,1)S(1)} %bitcast.7), channel_id=1, source_target_pairs={{0,36},{12,0},{24,12},{36,24},{1,37},{13,1},{25,13},{37,25},{2,38}... | collective-permute-start | bytes 1179656 | tf_op jit(solution)/shard_map/ppermute | solution.py:169
  66.1 0.0 collective-permute-done.4.refs_3_
  66.1 3.9 %collective-permute-start.5 = (bf16[6,2,16,1024]{3,2,1,0:T(8,128)(2,1)S(1)}, bf16[6,2,16,1024]{3,2,1,0:T(8,128)(2,1)S(1)}, u32[]{:S(2)}, u32[]{:S(2)}) collective-permute-start(bf16[6,2,16,1024]{3,2,1,0:T(8,128)(2,1)S(1)} %collective-permute-done.4.refs_3_), channel_id=1, source_target_pairs={{0,36},{12,0},{24,12},{36,24},{1,37},{13,1},{25,13},{37,25},{2,38}... | collective-permute-start | bytes 1179656 | tf_op jit(solution)/shard_map/ppermute | solution.py:171
  70.1 0.8 collective-permute-done.2.refs_2_
  70.9 1.9 %collective-permute-start.3 = (bf16[6,2,16,1024]{3,2,1,0:T(8,128)(2,1)S(1)}, bf16[6,2,16,1024]{3,2,1,0:T(8,128)(2,1)S(1)}, u32[]{:S(2)}, u32[]{:S(2)}) collective-permute-start(bf16[6,2,16,1024]{3,2,1,0:T(8,128)(2,1)S(1)} %collective-permute-done.2.refs_2_), channel_id=1, source_target_pairs={{0,12},{12,24},{24,36},{36,0},{1,13},{13,25},{25,37},{37,1},{2,14}... | collective-permute-start | bytes 1179656 | tf_op jit(solution)/shard_map/ppermute | solution.py:170
  73.4 0.0 copy-done
  73.4 0.0 copy-done.1
  73.4 4.8 %attend.2 = (f32[8,1,1024]{2,1,0:T(1,128)S(1)}, f32[8,1,1024]{2,1,0:T(1,128)S(1)}, f32[8,128,1024]{2,1,0:T(8,128)S(1)}) custom-call(f32[1]{0:T(128)S(6)} %copy.7.gate_ref, bf16[1,128,8192]{2,1,0:T(8,128)(2,1)S(1)} %copy-done, s32[1,128]{1,0:T(1,128)S(1)} %bitcast.12, bf16[6,2,16,1024]{3,2,1,0:T(8,128)(2,1)S(1)} %bitcast.8, ...), custom_call_target="tpu_custom_call" | custom-call | flops 1610612736 | bytes 10485760 | tf_op jit(solution)/shard_map/attend/pallas_call | solution.py:138
  78.3 0.2 collective-permute-done.refs_0_
  78.5 0.0 collective-permute-done.1.refs_1_
  78.5 0.8 collective-permute-done.5.refs_3_
  79.3 3.4 %collective-permute-done.3.refs_2_ = bf16[6,2,16,1024]{3,2,1,0:T(8,128)(2,1)S(1)} collective-permute-done((bf16[6,2,16,1024]{3,2,1,0:T(8,128)(2,1)S(1)}, bf16[6,2,16,1024]{3,2,1,0:T(8,128)(2,1)S(1)}, u32[]{:S(2)}, u32[]{:S(2)}) %collective-permute-start.3) | collective-permute-done | bytes 393248 | tf_op jit(solution)/shard_map/ppermute | solution.py:170
  82.7 6.3 %attend.3 = bf16[1,128,8192]{2,1,0:T(8,128)(2,1)} custom-call(f32[1]{0:T(128)S(6)} %copy.7.gate_ref, bf16[1,128,8192]{2,1,0:T(8,128)(2,1)S(1)} %copy-done, s32[1,128]{1,0:T(1,128)S(1)} %bitcast.13, bf16[6,2,16,1024]{3,2,1,0:T(8,128)(2,1)S(1)} %collective-permute-done.refs_0_, bf16[6,2,16,1024]{3,2,1,0:T(8,128)(2,1)S(1)} %collective-permute-done.1.refs_1_, ...), custom_call_target="tpu_custom_call" | custom-call | flops 1610612736 | bytes 10485760 | tf_op jit(solution)/shard_map/attend/pallas_call | solution.py:138
  (1 shorter events, 0.0 us)
Async XLA Ops:
  0.0 73.4 %copy-start = (bf16[1,128,8192]{2,1,0:T(8,128)(2,1)S(1)}, bf16[1,128,8192]{2,1,0:T(8,128)(2,1)}, u32[]{:S(2)}) copy-start(bf16[1,128,8192]{2,1,0:T(8,128)(2,1)} %q_ref.3) | copy-start | bytes 6291460
  0.0 73.4 %copy-start.1 = (s32[128]{0:T(128)S(1)}, s32[128]{0:T(128)}, u32[]{:S(2)}) copy-start(s32[128]{0:T(128)} %param.6) | copy-start | bytes 1540
  52.5 13.7 %collective-permute-start.4 = (bf16[6,2,16,1024]{3,2,1,0:T(8,128)(2,1)S(1)}, bf16[6,2,16,1024]{3,2,1,0:T(8,128)(2,1)S(1)}, u32[]{:S(2)}, u32[]{:S(2)}) collective-permute-start(bf16[6,2,16,1024]{3,2,1,0:T(8,128)(2,1)S(1)} %bitcast.9), channel_id=1, source_target_pairs={{0,36},{12,0},{24,12},{36,24},{1,37},{13,1},{25,13},{37,25},{2,38}... | collective-permute-start | bytes 1179656 | tf_op jit(solution)/shard_map/ppermute | solution.py:167
  57.1 13.7 %collective-permute-start.2 = (bf16[6,2,16,1024]{3,2,1,0:T(8,128)(2,1)S(1)}, bf16[6,2,16,1024]{3,2,1,0:T(8,128)(2,1)S(1)}, u32[]{:S(2)}, u32[]{:S(2)}) collective-permute-start(bf16[6,2,16,1024]{3,2,1,0:T(8,128)(2,1)S(1)} %bitcast.6), channel_id=1, source_target_pairs={{0,12},{12,24},{24,36},{36,0},{1,13},{13,25},{25,37},{37,1},{2,14}... | collective-permute-start | bytes 1179656 | tf_op jit(solution)/shard_map/ppermute | solution.py:166
  59.1 19.4 %collective-permute-start = (bf16[6,2,16,1024]{3,2,1,0:T(8,128)(2,1)S(1)}, bf16[6,2,16,1024]{3,2,1,0:T(8,128)(2,1)S(1)}, u32[]{:S(2)}, u32[]{:S(2)}) collective-permute-start(bf16[6,2,16,1024]{3,2,1,0:T(8,128)(2,1)S(1)} %bitcast.10), channel_id=1, source_target_pairs={{0,12},{12,24},{24,36},{36,0},{1,13},{13,25},{25,37},{37,1},{2,14}... | collective-permute-start | bytes 1179656 | tf_op jit(solution)/shard_map/ppermute | solution.py:168
  61.7 16.8 %collective-permute-start.1 = (bf16[6,2,16,1024]{3,2,1,0:T(8,128)(2,1)S(1)}, bf16[6,2,16,1024]{3,2,1,0:T(8,128)(2,1)S(1)}, u32[]{:S(2)}, u32[]{:S(2)}) collective-permute-start(bf16[6,2,16,1024]{3,2,1,0:T(8,128)(2,1)S(1)} %bitcast.7), channel_id=1, source_target_pairs={{0,36},{12,0},{24,12},{36,24},{1,37},{13,1},{25,13},{37,25},{2,38}... | collective-permute-start | bytes 1179656 | tf_op jit(solution)/shard_map/ppermute | solution.py:169
  66.1 13.1 %collective-permute-start.5 = (bf16[6,2,16,1024]{3,2,1,0:T(8,128)(2,1)S(1)}, bf16[6,2,16,1024]{3,2,1,0:T(8,128)(2,1)S(1)}, u32[]{:S(2)}, u32[]{:S(2)}) collective-permute-start(bf16[6,2,16,1024]{3,2,1,0:T(8,128)(2,1)S(1)} %collective-permute-done.4.refs_3_), channel_id=1, source_target_pairs={{0,36},{12,0},{24,12},{36,24},{1,37},{13,1},{25,13},{37,25},{2,38}... | collective-permute-start | bytes 1179656 | tf_op jit(solution)/shard_map/ppermute | solution.py:171
  70.9 11.8 %collective-permute-start.3 = (bf16[6,2,16,1024]{3,2,1,0:T(8,128)(2,1)S(1)}, bf16[6,2,16,1024]{3,2,1,0:T(8,128)(2,1)S(1)}, u32[]{:S(2)}, u32[]{:S(2)}) collective-permute-start(bf16[6,2,16,1024]{3,2,1,0:T(8,128)(2,1)S(1)} %collective-permute-done.2.refs_2_), channel_id=1, source_target_pairs={{0,12},{12,24},{24,36},{36,0},{1,13},{13,25},{25,37},{37,1},{2,14}... | collective-permute-start | bytes 1179656 | tf_op jit(solution)/shard_map/ppermute | solution.py:170

commit v4 on v3

--- a/solution.py
+++ b/solution.py
@@ -102,7 +102,7 @@
             store(k).start()
         return top
 
-    lax.fori_loop(0, KVH, head, scores(0, 0), unroll=4)
+    lax.fori_loop(0, KVH, head, scores(0, 0), unroll=8 if last else 4)
     if last:
         lax.fori_loop(0, KVH, lambda k, carry: (store(k).wait(), carry)[1], 0)
 
@@ -144,11 +144,6 @@
         input_output_aliases=aliases,
         name="attend",
         compiler_params=pltpu.CompilerParams(vmem_limit_bytes=VMEM_BYTES),
-        cost_estimate=pl.CostEstimate(
-            flops=4 * H * rows * total * HD,
-            bytes_accessed=2 * H * rows * HD + 8 * H * rows * HD,
-            transcendentals=H * rows * total,
-        ),
     )(*operands)
 
 
@@ -170,7 +165,8 @@
     low_far = lax.ppermute(low_left, "x", up)
     high_far = lax.ppermute(high_right, "x", down)
     state = attend(gate, queries, seen, (low, high, low_left, high_right), None, False)
-    return attend(gate, queries, seen, (high_left, low_right, low_far, high_far), state, True)
+    state = attend(gate, queries, seen, (high_left, low_right), state, False)
+    return attend(gate, queries, seen, (low_far, high_far), state, True)
 
 
 def solution(mesh):

time: 89.4 us -> 88 us (0.984)
  waiting for transfers between devices: 5.19 us -> 2.01 us
  Pallas kernels: 11.2 us -> 13.1 us
    ppermute x1, waiting for transfers between devices: 3.44 us -> 0.01 us  [body(): low_far = lax.ppermute(low_left, 'x', up)]
    ppermute x1, waiting for transfers between devices: 0.01 us -> 1.99 us  [body(): high_right = lax.ppermute(high, 'x', down)]
    pallas_call x2 -> x3, Pallas kernels: 11.2 us -> 13.1 us  [attend(): pl.pallas_call(functools.partial(attend_kernel, first, last, len(parts)),...]
    ppermute x1, starting transfers between devices: 1.92 us -> 3.4 us  [body(): low_left = lax.ppermute(low, 'x', up)]
    ppermute x1, starting transfers between devices: 4.67 us -> 3.65 us  [body(): high_right = lax.ppermute(high, 'x', down)]
    ppermute x1, starting transfers between devices: 4.4 us -> 3.46 us  [body(): low_right = lax.ppermute(low, 'x', down)]
  transfers between devices with their start and end apart: 6 -> 6, of which waited for: 4 -> 1; matrix products, arithmetic and copies ran while one was open for 0% -> 0% of each run, Pallas kernels for 5% -> 10%
where the time goes in v4:
time: 88 us; the launch traced here: 87.7 us
  blocking collectives  51.4 us (58%)
  starting transfers between devices  18.7 us (21%)
  Pallas kernels  13.1 us (15%)
  waiting for transfers between devices  2.01 us (2%)
  local copies, waits for them, and re-layouts  1.68 us (2%)
    all_gather x1, blocking collectives, body(): own = lax.all_gather(mine, 'z')  32.5 us
    all_to_all x1, blocking collectives, body(): mine = lax.all_to_all(sent, YRING, split_axis=0, concat_axis=0, tiled=True)  18.9 us
    pallas_call x3, Pallas kernels, attend(): pl.pallas_call(functools.partial(attend_kernel, first, last, len(parts)),...  13.1 us
    ppermute x1, starting transfers between devices, body(): high_right = lax.ppermute(high, 'x', down)  3.65 us
    ppermute x1, starting transfers between devices, body(): high_far = lax.ppermute(high_right, 'x', down)  3.65 us
    ppermute x1, starting transfers between devices, body(): low_right = lax.ppermute(low, 'x', down)  3.46 us
    ppermute x1, starting transfers between devices, body(): low_left = lax.ppermute(low, 'x', up)  3.4 us
    ppermute x1, starting transfers between devices, body(): high_left = lax.ppermute(high, 'x', up)  2.39 us
  transfers between devices with their start and end apart: 6, of which 1 were waited for; matrix products, arithmetic and copies ran while one was open for 0% of the time, Pallas kernels for 10%

profile of v4, /device:TPU:8, one launch (start us, length us, event | category | flops | bytes accessed | tf_op | source)
XLA Modules:
  0.0 87.7 jit_solution(8250764805477481055)
XLA Ops:
  0.0 0.0 copy-start
  0.0 0.9 %broadcast_in_dim.7 = bf16[8,2,2,1024]{3,2,1,0:T(2,128)(2,1)S(1)} broadcast(bf16[8,2,1024]{2,1,0:T(2,128)(2,1)} %bitcast.17), dimensions={0,2,3} | broadcast | bytes 98304 | tf_op jit(solution)/shard_map/broadcast_in_dim | solution.py:153
  0.9 18.9 %all_to_all.5 = bf16[16,2,1024]{2,1,0:T(2,128)(2,1)S(1)} all-to-all(bf16[16,2,1024]{2,1,0:T(2,128)(2,1)S(1)} %bitcast.16), channel_id=1, replica_groups=mesh['ylo'=4,'core'=2,'yhi'=2,'x'=4,'z'=12] {'ylo','core','yhi'}, dimensions={0} | all-to-all | bytes 131072 | tf_op jit(solution)/shard_map/all_to_all | solution.py:154
  19.9 32.5 %all-gather = bf16[24,16,1024]{2,1,0:T(8,128)(2,1)S(1)} all-gather(bf16[2,16,1024]{2,1,0:T(8,128)(2,1)S(1)} %copy.9), channel_id=2, replica_groups=mesh['ylo'=4,'core'=2,'yhi'=2,'x'=4,'z'=12] {'z'}, dimensions={0}, use_global_device_ids=true | all-gather | bytes 851968 | tf_op jit(solution)/shard_map/all_gather | solution.py:156
  52.4 0.1 fusion
  52.5 3.4 %collective-permute-start = (bf16[6,2,16,1024]{3,2,1,0:T(8,128)(2,1)S(1)}, bf16[6,2,16,1024]{3,2,1,0:T(8,128)(2,1)S(1)}, u32[]{:S(2)}, u32[]{:S(2)}) collective-permute-start(bf16[6,2,16,1024]{3,2,1,0:T(8,128)(2,1)S(1)} %bitcast.9), channel_id=1, source_target_pairs={{0,12},{12,24},{24,36},{36,0},{1,13},{13,25},{25,37},{37,1},{2,14}... | collective-permute-start | bytes 1179656 | tf_op jit(solution)/shard_map/ppermute | solution.py:161
  55.9 3.7 %collective-permute-start.2 = (bf16[6,2,16,1024]{3,2,1,0:T(8,128)(2,1)S(1)}, bf16[6,2,16,1024]{3,2,1,0:T(8,128)(2,1)S(1)}, u32[]{:S(2)}, u32[]{:S(2)}) collective-permute-start(bf16[6,2,16,1024]{3,2,1,0:T(8,128)(2,1)S(1)} %bitcast.6), channel_id=1, source_target_pairs={{0,36},{12,0},{24,12},{36,24},{1,37},{13,1},{25,13},{37,25},{2,38}... | collective-permute-start | bytes 1179656 | tf_op jit(solution)/shard_map/ppermute | solution.py:162
  59.5 3.5 %collective-permute-start.5 = (bf16[6,2,16,1024]{3,2,1,0:T(8,128)(2,1)S(1)}, bf16[6,2,16,1024]{3,2,1,0:T(8,128)(2,1)S(1)}, u32[]{:S(2)}, u32[]{:S(2)}) collective-permute-start(bf16[6,2,16,1024]{3,2,1,0:T(8,128)(2,1)S(1)} %bitcast.10), channel_id=1, source_target_pairs={{0,36},{12,0},{24,12},{36,24},{1,37},{13,1},{25,13},{37,25},{2,38}... | collective-permute-start | bytes 1179656 | tf_op jit(solution)/shard_map/ppermute | solution.py:164
  63.0 2.4 %collective-permute-start.4 = (bf16[6,2,16,1024]{3,2,1,0:T(8,128)(2,1)S(1)}, bf16[6,2,16,1024]{3,2,1,0:T(8,128)(2,1)S(1)}, u32[]{:S(2)}, u32[]{:S(2)}) collective-permute-start(bf16[6,2,16,1024]{3,2,1,0:T(8,128)(2,1)S(1)} %bitcast.7), channel_id=1, source_target_pairs={{0,12},{12,24},{24,36},{36,0},{1,13},{13,25},{25,37},{37,1},{2,14}... | collective-permute-start | bytes 1179656 | tf_op jit(solution)/shard_map/ppermute | solution.py:163
  65.4 0.0 collective-permute-done.refs_2_
  65.4 2.2 %collective-permute-start.1 = (bf16[6,2,16,1024]{3,2,1,0:T(8,128)(2,1)S(1)}, bf16[6,2,16,1024]{3,2,1,0:T(8,128)(2,1)S(1)}, u32[]{:S(2)}, u32[]{:S(2)}) collective-permute-start(bf16[6,2,16,1024]{3,2,1,0:T(8,128)(2,1)S(1)} %collective-permute-done.refs_2_), channel_id=1, source_target_pairs={{0,12},{12,24},{24,36},{36,0},{1,13},{13,25},{25,37},{37,1},{2,14}... | collective-permute-start | bytes 1179656 | tf_op jit(solution)/shard_map/ppermute | solution.py:165
  67.6 2.0 %collective-permute-done.2.refs_3_ = bf16[6,2,16,1024]{3,2,1,0:T(8,128)(2,1)S(1)} collective-permute-done((bf16[6,2,16,1024]{3,2,1,0:T(8,128)(2,1)S(1)}, bf16[6,2,16,1024]{3,2,1,0:T(8,128)(2,1)S(1)}, u32[]{:S(2)}, u32[]{:S(2)}) %collective-permute-start.2) | collective-permute-done | bytes 393248 | tf_op jit(solution)/shard_map/ppermute | solution.py:162
  69.6 3.7 %collective-permute-start.3 = (bf16[6,2,16,1024]{3,2,1,0:T(8,128)(2,1)S(1)}, bf16[6,2,16,1024]{3,2,1,0:T(8,128)(2,1)S(1)}, u32[]{:S(2)}, u32[]{:S(2)}) collective-permute-start(bf16[6,2,16,1024]{3,2,1,0:T(8,128)(2,1)S(1)} %collective-permute-done.2.refs_3_), channel_id=1, source_target_pairs={{0,36},{12,0},{24,12},{36,24},{1,37},{13,1},{25,13},{37,25},{2,38}... | collective-permute-start | bytes 1179656 | tf_op jit(solution)/shard_map/ppermute | solution.py:166
  73.9 0.0 copy-done
  73.9 0.0 copy-start.1
  73.9 0.6 copy-done.1
  74.6 4.8 %attend.3 = (f32[8,1,1024]{2,1,0:T(1,128)S(1)}, f32[8,1,1024]{2,1,0:T(1,128)S(1)}, f32[8,128,1024]{2,1,0:T(8,128)S(1)}) custom-call(f32[1]{0:T(128)S(6)} %copy.13.gate_ref, bf16[1,128,8192]{2,1,0:T(8,128)(2,1)S(1)} %copy-done, s32[1,128]{1,0:T(1,128)S(1)} %bitcast.12, bf16[6,2,16,1024]{3,2,1,0:T(8,128)(2,1)S(1)} %bitcast.11, ...), custom_call_target="tpu_custom_call" | custom-call | tf_op jit(solution)/shard_map/attend/pallas_call | solution.py:138
  79.4 0.0 collective-permute-done.5.refs_1_
  79.4 0.0 collective-permute-done.4.refs_0_
  79.4 3.7 %attend.4 = (f32[8,1,1024]{2,1,0:T(1,128)S(1)}, f32[8,1,1024]{2,1,0:T(1,128)S(1)}, f32[8,128,1024]{2,1,0:T(8,128)S(1)}) custom-call(f32[1]{0:T(128)S(6)} %copy.13.gate_ref, bf16[1,128,8192]{2,1,0:T(8,128)(2,1)S(1)} %copy-done, s32[1,128]{1,0:T(1,128)S(1)} %bitcast.13, ...), custom_call_target="tpu_custom_call", output_to_operand_aliasing={{0}: (5, {}), {1}: (6, {}), {2}: (7, {})} | custom-call | tf_op jit(solution)/shard_map/attend/pallas_call | solution.py:138
  83.1 0.0 collective-permute-done.1.refs_0_
  83.1 0.0 collective-permute-done.3.refs_1_
  83.1 4.6 %attend.5 = bf16[1,128,8192]{2,1,0:T(8,128)(2,1)} custom-call(f32[1]{0:T(128)S(6)} %copy.13.gate_ref, bf16[1,128,8192]{2,1,0:T(8,128)(2,1)S(1)} %copy-done, s32[1,128]{1,0:T(1,128)S(1)} %bitcast.14, bf16[6,2,16,1024]{3,2,1,0:T(8,128)(2,1)S(1)} %collective-permute-done.1.refs_0_, bf16[6,2,16,1024]{3,2,1,0:T(8,128)(2,1)S(1)} %collective-permute-done.3.refs_1_, ...), custom_call_target="tpu_custom_call" | custom-call | tf_op jit(solution)/shard_map/attend/pallas_call | solution.py:138
  (1 shorter events, 0.0 us)
Async XLA Ops:
  0.0 73.9 %copy-start = (bf16[1,128,8192]{2,1,0:T(8,128)(2,1)S(1)}, bf16[1,128,8192]{2,1,0:T(8,128)(2,1)}, u32[]{:S(2)}) copy-start(bf16[1,128,8192]{2,1,0:T(8,128)(2,1)} %q_ref.5) | copy-start | bytes 6291460
  52.5 12.9 %collective-permute-start = (bf16[6,2,16,1024]{3,2,1,0:T(8,128)(2,1)S(1)}, bf16[6,2,16,1024]{3,2,1,0:T(8,128)(2,1)S(1)}, u32[]{:S(2)}, u32[]{:S(2)}) collective-permute-start(bf16[6,2,16,1024]{3,2,1,0:T(8,128)(2,1)S(1)} %bitcast.9), channel_id=1, source_target_pairs={{0,12},{12,24},{24,36},{36,0},{1,13},{13,25},{25,37},{37,1},{2,14}... | collective-permute-start | bytes 1179656 | tf_op jit(solution)/shard_map/ppermute | solution.py:161
  55.9 13.7 %collective-permute-start.2 = (bf16[6,2,16,1024]{3,2,1,0:T(8,128)(2,1)S(1)}, bf16[6,2,16,1024]{3,2,1,0:T(8,128)(2,1)S(1)}, u32[]{:S(2)}, u32[]{:S(2)}) collective-permute-start(bf16[6,2,16,1024]{3,2,1,0:T(8,128)(2,1)S(1)} %bitcast.6), channel_id=1, source_target_pairs={{0,36},{12,0},{24,12},{36,24},{1,37},{13,1},{25,13},{37,25},{2,38}... | collective-permute-start | bytes 1179656 | tf_op jit(solution)/shard_map/ppermute | solution.py:162
  59.5 19.8 %collective-permute-start.5 = (bf16[6,2,16,1024]{3,2,1,0:T(8,128)(2,1)S(1)}, bf16[6,2,16,1024]{3,2,1,0:T(8,128)(2,1)S(1)}, u32[]{:S(2)}, u32[]{:S(2)}) collective-permute-start(bf16[6,2,16,1024]{3,2,1,0:T(8,128)(2,1)S(1)} %bitcast.10), channel_id=1, source_target_pairs={{0,36},{12,0},{24,12},{36,24},{1,37},{13,1},{25,13},{37,25},{2,38}... | collective-permute-start | bytes 1179656 | tf_op jit(solution)/shard_map/ppermute | solution.py:164
  63.0 16.4 %collective-permute-start.4 = (bf16[6,2,16,1024]{3,2,1,0:T(8,128)(2,1)S(1)}, bf16[6,2,16,1024]{3,2,1,0:T(8,128)(2,1)S(1)}, u32[]{:S(2)}, u32[]{:S(2)}) collective-permute-start(bf16[6,2,16,1024]{3,2,1,0:T(8,128)(2,1)S(1)} %bitcast.7), channel_id=1, source_target_pairs={{0,12},{12,24},{24,36},{36,0},{1,13},{13,25},{25,37},{37,1},{2,14}... | collective-permute-start | bytes 1179656 | tf_op jit(solution)/shard_map/ppermute | solution.py:163
  65.4 17.7 %collective-permute-start.1 = (bf16[6,2,16,1024]{3,2,1,0:T(8,128)(2,1)S(1)}, bf16[6,2,16,1024]{3,2,1,0:T(8,128)(2,1)S(1)}, u32[]{:S(2)}, u32[]{:S(2)}) collective-permute-start(bf16[6,2,16,1024]{3,2,1,0:T(8,128)(2,1)S(1)} %collective-permute-done.refs_2_), channel_id=1, source_target_pairs={{0,12},{12,24},{24,36},{36,0},{1,13},{13,25},{25,37},{37,1},{2,14}... | collective-permute-start | bytes 1179656 | tf_op jit(solution)/shard_map/ppermute | solution.py:165
  69.6 13.5 %collective-permute-start.3 = (bf16[6,2,16,1024]{3,2,1,0:T(8,128)(2,1)S(1)}, bf16[6,2,16,1024]{3,2,1,0:T(8,128)(2,1)S(1)}, u32[]{:S(2)}, u32[]{:S(2)}) collective-permute-start(bf16[6,2,16,1024]{3,2,1,0:T(8,128)(2,1)S(1)} %collective-permute-done.2.refs_3_), channel_id=1, source_target_pairs={{0,36},{12,0},{24,12},{36,24},{1,37},{13,1},{25,13},{37,25},{2,38}... | collective-permute-start | bytes 1179656 | tf_op jit(solution)/shard_map/ppermute | solution.py:166
  73.9 0.7 copy-start.1

commit v5 on v4

--- a/solution.py
+++ b/solution.py
@@ -165,8 +165,8 @@
     low_far = lax.ppermute(low_left, "x", up)
     high_far = lax.ppermute(high_right, "x", down)
     state = attend(gate, queries, seen, (low, high, low_left, high_right), None, False)
-    state = attend(gate, queries, seen, (high_left, low_right), state, False)
-    return attend(gate, queries, seen, (low_far, high_far), state, True)
+    state = attend(gate, queries, seen, (high_left, low_right, low_far), state, False)
+    return attend(gate, queries, seen, (high_far,), state, True)
 
 
 def solution(mesh):

time: 88 us -> 89.5 us (1.017)
  starting transfers between devices: 18.7 us -> 21.4 us
  waiting for transfers between devices: 2.01 us -> 0.57 us
    ppermute x1, waiting for transfers between devices: 1.99 us -> 0.01 us  [body(): high_right = lax.ppermute(high, 'x', down)]
    ppermute x1, starting transfers between devices: 3.46 us -> 4.86 us  [body(): low_right = lax.ppermute(low, 'x', down)]
    ppermute x1, starting transfers between devices: 3.65 us -> 4.73 us  [body(): high_far = lax.ppermute(high_right, 'x', down)]
  transfers between devices with their start and end apart: 6 -> 6, of which waited for: 1 -> 1; matrix products, arithmetic and copies ran while one was open for 0% -> 0% of each run, Pallas kernels for 10% -> 11%
where the time goes in v5:
time: 89.5 us; the launch traced here: 89.2 us
  blocking collectives  51.4 us (57%)
  starting transfers between devices  21.4 us (24%)
  Pallas kernels  13.3 us (15%)
  local copies, waits for them, and re-layouts  1.68 us (2%)
    all_gather x1, blocking collectives, body(): own = lax.all_gather(mine, 'z')  32.5 us
    all_to_all x1, blocking collectives, body(): mine = lax.all_to_all(sent, YRING, split_axis=0, concat_axis=0, tiled=True)  18.9 us
    pallas_call x3, Pallas kernels, attend(): pl.pallas_call(functools.partial(attend_kernel, first, last, len(parts)),...  13.3 us
    ppermute x1, starting transfers between devices, body(): low_right = lax.ppermute(low, 'x', down)  4.86 us
    ppermute x1, starting transfers between devices, body(): high_far = lax.ppermute(high_right, 'x', down)  4.73 us
    ppermute x1, starting transfers between devices, body(): high_right = lax.ppermute(high, 'x', down)  3.65 us
    ppermute x1, starting transfers between devices, body(): low_left = lax.ppermute(low, 'x', up)  3.4 us
    ppermute x1, starting transfers between devices, body(): low_far = lax.ppermute(low_left, 'x', up)  2.58 us
  transfers between devices with their start and end apart: 6, of which 1 were waited for; matrix products, arithmetic and copies ran while one was open for 0% of the time, Pallas kernels for 11%

profile of v5, /device:TPU:8, one launch (start us, length us, event | category | flops | bytes accessed | tf_op | source)
XLA Modules:
  0.0 89.2 jit_solution(17929707635316883297)
XLA Ops:
  0.0 0.0 copy-start
  0.0 0.9 %broadcast_in_dim.7 = bf16[8,2,2,1024]{3,2,1,0:T(2,128)(2,1)S(1)} broadcast(bf16[8,2,1024]{2,1,0:T(2,128)(2,1)} %bitcast.17), dimensions={0,2,3} | broadcast | bytes 98304 | tf_op jit(solution)/shard_map/broadcast_in_dim | solution.py:153
  0.9 18.9 %all_to_all.5 = bf16[16,2,1024]{2,1,0:T(2,128)(2,1)S(1)} all-to-all(bf16[16,2,1024]{2,1,0:T(2,128)(2,1)S(1)} %bitcast.16), channel_id=1, replica_groups=mesh['ylo'=4,'core'=2,'yhi'=2,'x'=4,'z'=12] {'ylo','core','yhi'}, dimensions={0} | all-to-all | bytes 131072 | tf_op jit(solution)/shard_map/all_to_all | solution.py:154
  19.9 32.5 %all-gather = bf16[24,16,1024]{2,1,0:T(8,128)(2,1)S(1)} all-gather(bf16[2,16,1024]{2,1,0:T(8,128)(2,1)S(1)} %copy.9), channel_id=2, replica_groups=mesh['ylo'=4,'core'=2,'yhi'=2,'x'=4,'z'=12] {'z'}, dimensions={0}, use_global_device_ids=true | all-gather | bytes 851968 | tf_op jit(solution)/shard_map/all_gather | solution.py:156
  52.4 0.1 fusion
  52.5 3.4 %collective-permute-start.4 = (bf16[6,2,16,1024]{3,2,1,0:T(8,128)(2,1)S(1)}, bf16[6,2,16,1024]{3,2,1,0:T(8,128)(2,1)S(1)}, u32[]{:S(2)}, u32[]{:S(2)}) collective-permute-start(bf16[6,2,16,1024]{3,2,1,0:T(8,128)(2,1)S(1)} %bitcast.6), channel_id=1, source_target_pairs={{0,12},{12,24},{24,36},{36,0},{1,13},{13,25},{25,37},{37,1},{2,14}... | collective-permute-start | bytes 1179656 | tf_op jit(solution)/shard_map/ppermute | solution.py:161
  55.9 3.7 %collective-permute-start = (bf16[6,2,16,1024]{3,2,1,0:T(8,128)(2,1)S(1)}, bf16[6,2,16,1024]{3,2,1,0:T(8,128)(2,1)S(1)}, u32[]{:S(2)}, u32[]{:S(2)}) collective-permute-start(bf16[6,2,16,1024]{3,2,1,0:T(8,128)(2,1)S(1)} %bitcast.9), channel_id=1, source_target_pairs={{0,36},{12,0},{24,12},{36,24},{1,37},{13,1},{25,13},{37,25},{2,38}... | collective-permute-start | bytes 1179656 | tf_op jit(solution)/shard_map/ppermute | solution.py:162
  59.5 2.2 %collective-permute-start.2 = (bf16[6,2,16,1024]{3,2,1,0:T(8,128)(2,1)S(1)}, bf16[6,2,16,1024]{3,2,1,0:T(8,128)(2,1)S(1)}, u32[]{:S(2)}, u32[]{:S(2)}) collective-permute-start(bf16[6,2,16,1024]{3,2,1,0:T(8,128)(2,1)S(1)} %bitcast.10), channel_id=1, source_target_pairs={{0,12},{12,24},{24,36},{36,0},{1,13},{13,25},{25,37},{37,1},{2,14}... | collective-permute-start | bytes 1179656 | tf_op jit(solution)/shard_map/ppermute | solution.py:163
  61.7 4.9 %collective-permute-start.3 = (bf16[6,2,16,1024]{3,2,1,0:T(8,128)(2,1)S(1)}, bf16[6,2,16,1024]{3,2,1,0:T(8,128)(2,1)S(1)}, u32[]{:S(2)}, u32[]{:S(2)}) collective-permute-start(bf16[6,2,16,1024]{3,2,1,0:T(8,128)(2,1)S(1)} %bitcast.7), channel_id=1, source_target_pairs={{0,36},{12,0},{24,12},{36,24},{1,37},{13,1},{25,13},{37,25},{2,38}... | collective-permute-start | bytes 1179656 | tf_op jit(solution)/shard_map/ppermute | solution.py:164
  66.6 0.6 collective-permute-done.4.refs_2_
  67.1 2.6 %collective-permute-start.5 = (bf16[6,2,16,1024]{3,2,1,0:T(8,128)(2,1)S(1)}, bf16[6,2,16,1024]{3,2,1,0:T(8,128)(2,1)S(1)}, u32[]{:S(2)}, u32[]{:S(2)}) collective-permute-start(bf16[6,2,16,1024]{3,2,1,0:T(8,128)(2,1)S(1)} %collective-permute-done.4.refs_2_), channel_id=1, source_target_pairs={{0,12},{12,24},{24,36},{36,0},{1,13},{13,25},{25,37},{37,1},{2,14}... | collective-permute-start | bytes 1179656 | tf_op jit(solution)/shard_map/ppermute | solution.py:165
  69.7 0.0 collective-permute-done.refs_3_
  69.7 4.7 %collective-permute-start.1 = (bf16[6,2,16,1024]{3,2,1,0:T(8,128)(2,1)S(1)}, bf16[6,2,16,1024]{3,2,1,0:T(8,128)(2,1)S(1)}, u32[]{:S(2)}, u32[]{:S(2)}) collective-permute-start(bf16[6,2,16,1024]{3,2,1,0:T(8,128)(2,1)S(1)} %collective-permute-done.refs_3_), channel_id=1, source_target_pairs={{0,36},{12,0},{24,12},{36,24},{1,37},{13,1},{25,13},{37,25},{2,38}... | collective-permute-start | bytes 1179656 | tf_op jit(solution)/shard_map/ppermute | solution.py:166
  75.1 0.0 copy-done
  75.1 0.0 copy-start.1
  75.1 0.6 copy-done.1
  75.8 4.8 %attend.3 = (f32[8,1,1024]{2,1,0:T(1,128)S(1)}, f32[8,1,1024]{2,1,0:T(1,128)S(1)}, f32[8,128,1024]{2,1,0:T(8,128)S(1)}) custom-call(f32[1]{0:T(128)S(6)} %copy.13.gate_ref, bf16[1,128,8192]{2,1,0:T(8,128)(2,1)S(1)} %copy-done, s32[1,128]{1,0:T(1,128)S(1)} %bitcast.12, bf16[6,2,16,1024]{3,2,1,0:T(8,128)(2,1)S(1)} %bitcast.8, ...), custom_call_target="tpu_custom_call" | custom-call | tf_op jit(solution)/shard_map/attend/pallas_call | solution.py:138
  80.6 0.0 collective-permute-done.2.refs_0_
  80.6 0.0 collective-permute-done.3.refs_1_
  80.6 0.0 collective-permute-done.5.refs_2_
  80.6 4.6 %attend.4 = (f32[8,1,1024]{2,1,0:T(1,128)S(1)}, f32[8,1,1024]{2,1,0:T(1,128)S(1)}, f32[8,128,1024]{2,1,0:T(8,128)S(1)}) custom-call(f32[1]{0:T(128)S(6)} %copy.13.gate_ref, bf16[1,128,8192]{2,1,0:T(8,128)(2,1)S(1)} %copy-done, s32[1,128]{1,0:T(1,128)S(1)} %bitcast.13, ...), custom_call_target="tpu_custom_call", output_to_operand_aliasing={{0}: (6, {}), {1}: (7, {}), {2}: (8, {})} | custom-call | tf_op jit(solution)/shard_map/attend/pallas_call | solution.py:138
  85.2 0.0 collective-permute-done.1.refs_0_
  85.2 3.9 %attend.5 = bf16[1,128,8192]{2,1,0:T(8,128)(2,1)} custom-call(f32[1]{0:T(128)S(6)} %copy.13.gate_ref, bf16[1,128,8192]{2,1,0:T(8,128)(2,1)S(1)} %copy-done, s32[1,128]{1,0:T(1,128)S(1)} %bitcast.14, bf16[6,2,16,1024]{3,2,1,0:T(8,128)(2,1)S(1)} %collective-permute-done.1.refs_0_, f32[8,1,1024]{2,1,0:T(1,128)S(1)} %get-tuple-element.14.refs_1_, ...), custom_call_target="tpu_custom_call" | custom-call | tf_op jit(solution)/shard_map/attend/pallas_call | solution.py:138
  (1 shorter events, 0.0 us)
Async XLA Ops:
  0.0 75.1 %copy-start = (bf16[1,128,8192]{2,1,0:T(8,128)(2,1)S(1)}, bf16[1,128,8192]{2,1,0:T(8,128)(2,1)}, u32[]{:S(2)}) copy-start(bf16[1,128,8192]{2,1,0:T(8,128)(2,1)} %q_ref.5) | copy-start | bytes 6291460
  52.5 14.7 %collective-permute-start.4 = (bf16[6,2,16,1024]{3,2,1,0:T(8,128)(2,1)S(1)}, bf16[6,2,16,1024]{3,2,1,0:T(8,128)(2,1)S(1)}, u32[]{:S(2)}, u32[]{:S(2)}) collective-permute-start(bf16[6,2,16,1024]{3,2,1,0:T(8,128)(2,1)S(1)} %bitcast.6), channel_id=1, source_target_pairs={{0,12},{12,24},{24,36},{36,0},{1,13},{13,25},{25,37},{37,1},{2,14}... | collective-permute-start | bytes 1179656 | tf_op jit(solution)/shard_map/ppermute | solution.py:161
  55.9 13.9 %collective-permute-start = (bf16[6,2,16,1024]{3,2,1,0:T(8,128)(2,1)S(1)}, bf16[6,2,16,1024]{3,2,1,0:T(8,128)(2,1)S(1)}, u32[]{:S(2)}, u32[]{:S(2)}) collective-permute-start(bf16[6,2,16,1024]{3,2,1,0:T(8,128)(2,1)S(1)} %bitcast.9), channel_id=1, source_target_pairs={{0,36},{12,0},{24,12},{36,24},{1,37},{13,1},{25,13},{37,25},{2,38}... | collective-permute-start | bytes 1179656 | tf_op jit(solution)/shard_map/ppermute | solution.py:162
  59.5 21.1 %collective-permute-start.2 = (bf16[6,2,16,1024]{3,2,1,0:T(8,128)(2,1)S(1)}, bf16[6,2,16,1024]{3,2,1,0:T(8,128)(2,1)S(1)}, u32[]{:S(2)}, u32[]{:S(2)}) collective-permute-start(bf16[6,2,16,1024]{3,2,1,0:T(8,128)(2,1)S(1)} %bitcast.10), channel_id=1, source_target_pairs={{0,12},{12,24},{24,36},{36,0},{1,13},{13,25},{25,37},{37,1},{2,14}... | collective-permute-start | bytes 1179656 | tf_op jit(solution)/shard_map/ppermute | solution.py:163
  61.7 18.9 %collective-permute-start.3 = (bf16[6,2,16,1024]{3,2,1,0:T(8,128)(2,1)S(1)}, bf16[6,2,16,1024]{3,2,1,0:T(8,128)(2,1)S(1)}, u32[]{:S(2)}, u32[]{:S(2)}) collective-permute-start(bf16[6,2,16,1024]{3,2,1,0:T(8,128)(2,1)S(1)} %bitcast.7), channel_id=1, source_target_pairs={{0,36},{12,0},{24,12},{36,24},{1,37},{13,1},{25,13},{37,25},{2,38}... | collective-permute-start | bytes 1179656 | tf_op jit(solution)/shard_map/ppermute | solution.py:164
  67.1 13.5 %collective-permute-start.5 = (bf16[6,2,16,1024]{3,2,1,0:T(8,128)(2,1)S(1)}, bf16[6,2,16,1024]{3,2,1,0:T(8,128)(2,1)S(1)}, u32[]{:S(2)}, u32[]{:S(2)}) collective-permute-start(bf16[6,2,16,1024]{3,2,1,0:T(8,128)(2,1)S(1)} %collective-permute-done.4.refs_2_), channel_id=1, source_target_pairs={{0,12},{12,24},{24,36},{36,0},{1,13},{13,25},{25,37},{37,1},{2,14}... | collective-permute-start | bytes 1179656 | tf_op jit(solution)/shard_map/ppermute | solution.py:165
  69.7 15.5 %collective-permute-start.1 = (bf16[6,2,16,1024]{3,2,1,0:T(8,128)(2,1)S(1)}, bf16[6,2,16,1024]{3,2,1,0:T(8,128)(2,1)S(1)}, u32[]{:S(2)}, u32[]{:S(2)}) collective-permute-start(bf16[6,2,16,1024]{3,2,1,0:T(8,128)(2,1)S(1)} %collective-permute-done.refs_3_), channel_id=1, source_target_pairs={{0,36},{12,0},{24,12},{36,24},{1,37},{13,1},{25,13},{37,25},{2,38}... | collective-permute-start | bytes 1179656 | tf_op jit(solution)/shard_map/ppermute | solution.py:166
  75.1 0.7 copy-start.1
